TPU v7x, 128 devices: a whole 4x4x4 slice. The times are simulated.
128 devices in a mesh: wall: 16 (over y, z), span: 4 (over x), stream: 2 (over core).
Axes of the slice: x: 4, y: 4, z: 4, core: 2. Of those that a mesh axis runs over, the one named last changes fastest.
Arguments:
- conserved: float32 [5, 32, 1536, 512], P(None, 'stream', 'wall', 'span'), may hold values from -6 to 6
- wall_metric: float32 [32, 1536, 512], P('stream', 'wall', 'span'), may hold values from 0.5 to 4
- span_metric: float32 [32, 1536, 512], P('stream', 'wall', 'span'), may hold values from 0.5 to 4
Outputs:
- wall_slope: float32 [5, 32, 1536, 512], P(None, 'stream', 'wall', 'span')
- span_slope: float32 [5, 32, 1536, 512], P(None, 'stream', 'wall', 'span')
All inputs are finite; a program needn't handle non-finite values.
Results may differ from a plain program's by a relative error of at most 0.0003.
Values sent between devices are 32-bit elements; how exact they have to be, the bound alone decides.
No kernel may reach another device: no remote copies, remote signals or barrier semaphores. Data moves between devices by JAX's collectives and lax.ppermute only.
A program may use at most 128 MiB of HBM per device.

v0:
```python
import jax
import jax.numpy as jnp
import numpy as np
from jax import lax
from jax.sharding import PartitionSpec as P

HIGHEST_MODE = lax.Precision.HIGHEST
band_alpha = 0.4995


def line_coefficients(length_all):
    lower_band = np.full(length_all, band_alpha)
    lower_band[1] = 0.25
    lower_band[length_all - 2] = 0.25
    lower_band[0] = 0.0
    lower_band[length_all - 1] = 0.0
    scales = np.zeros(length_all)
    pivots = np.zeros(length_all)
    previous = 0.0
    for row_idx in range(length_all):
        scales[row_idx] = 1.0 / (1.0 - lower_band[row_idx] * previous)
        pivots[row_idx] = lower_band[row_idx] * scales[row_idx]
        previous = pivots[row_idx]
    near_coef = (band_alpha + 2.0) / 3.0
    far_coef = (4.0 * band_alpha - 1.0) / 12.0
    weights = np.zeros((5, length_all))
    weights[:, :] = np.array([-far_coef, -near_coef, 0.0, near_coef, far_coef])[:, None]
    weights[:, 1] = [0.0, -0.75, 0.0, 0.75, 0.0]
    weights[:, length_all - 2] = [0.0, -0.75, 0.0, 0.75, 0.0]
    weights[:, 0] = [0.0, 0.0, -1.5, 2.0, -0.5]
    weights[:, length_all - 1] = [0.5, -2.0, 1.5, 0.0, 0.0]
    return (lower_band, scales, pivots, weights)


def block_tables(pieces, block_len):
    length_all = pieces * block_len
    lower_band, scales, pivots, weights = line_coefficients(length_all)
    down_maps = np.zeros((pieces, block_len, block_len))
    enter_gain = np.zeros((pieces, block_len))
    back_maps = np.zeros((pieces, block_len, block_len))
    leave_gain = np.zeros((pieces, block_len))
    for piece_idx in range(pieces):
        base_row = piece_idx * block_len
        row_now = np.zeros(block_len)
        running = 1.0
        for step_idx in range(block_len):
            factor = -lower_band[base_row + step_idx] * scales[base_row + step_idx]
            row_now = factor * row_now
            row_now[step_idx] += 1.0
            down_maps[piece_idx, step_idx] = row_now * scales[base_row : base_row + block_len]
            running = factor * running
            enter_gain[piece_idx, step_idx] = running
        row_now = np.zeros(block_len)
        running = 1.0
        for step_idx in range(block_len - 1, -1, -1):
            factor = -pivots[base_row + step_idx]
            row_now = factor * row_now
            row_now[step_idx] += 1.0
            back_maps[piece_idx, step_idx] = row_now
            running = factor * running
            leave_gain[piece_idx, step_idx] = running
    return tuple(
        (
            jnp.asarray(table, jnp.float32)
            for table in (weights, down_maps, enter_gain, back_maps, leave_gain)
        )
    )


def compose(earlier, later):
    return (later[0] * earlier[0], later[0] * earlier[1] + later[1])


def stencil(padded, weights, block_len, line_dim):
    right_side = 0.0
    for offset in range(5):
        shifted = lax.slice_in_dim(padded, offset, offset + block_len, axis=line_dim)
        dims_list = [1, 1, 1, 1]
        dims_list[line_dim] = block_len
        right_side = right_side + weights[offset].reshape(dims_list) * shifted
    return right_side


def local_chain(factor, values, axis_pos, reverse):
    pieces = factor.shape[0]
    dims_list = [1] * values.ndim
    dims_list[axis_pos] = pieces
    factors = jnp.broadcast_to(factor.reshape(dims_list), values.shape)
    _, inclusive = lax.associative_scan(compose, (factors, values), reverse=reverse, axis=axis_pos)
    empty = jnp.zeros_like(lax.slice_in_dim(values, 0, 1, axis=axis_pos))
    if reverse:
        return jnp.concatenate(
            [lax.slice_in_dim(inclusive, 1, pieces, axis=axis_pos), empty], axis=axis_pos
        )
    return jnp.concatenate(
        [empty, lax.slice_in_dim(inclusive, 0, pieces - 1, axis=axis_pos)], axis=axis_pos
    )


def wall_whole_lines(line_data):
    pieces = lax.axis_size("wall")
    fields, planes, length_all, columns = line_data.shape
    block_len = length_all // pieces
    weights, down_maps, enter_gain, back_maps, leave_gain = block_tables(pieces, block_len)
    padded = jnp.pad(line_data, ((0, 0), (0, 0), (2, 2), (0, 0)))
    right_side = stencil(padded, weights, length_all, 2)
    blocked = right_side.reshape(fields, planes, pieces, block_len, columns)
    local_part = jnp.einsum("kij,fqkjs->fqkis", down_maps, blocked, precision=HIGHEST_MODE)
    inflow = local_chain(enter_gain[:, -1], local_part[:, :, :, -1, :], 2, False)
    reduced = local_part + enter_gain[None, None, :, :, None] * inflow[:, :, :, None, :]
    swept = jnp.einsum("kij,fqkjs->fqkis", back_maps, reduced, precision=HIGHEST_MODE)
    outflow = local_chain(leave_gain[:, 0], swept[:, :, :, 0, :], 2, True)
    slopes = swept + leave_gain[None, None, :, :, None] * outflow[:, :, :, None, :]
    slopes = slopes.reshape(fields, planes, length_all, columns)
    return lax.all_to_all(slopes, "wall", split_axis=2, concat_axis=1, tiled=True)


def span_whole_lines(line_data):
    pieces = lax.axis_size("span")
    fields, planes, rows_here, length_all = line_data.shape
    block_len = length_all // pieces
    weights, down_maps, enter_gain, back_maps, leave_gain = block_tables(pieces, block_len)
    padded = jnp.pad(line_data, ((0, 0), (0, 0), (0, 0), (2, 2)))
    right_side = stencil(padded, weights, length_all, 3)
    blocked = right_side.reshape(fields, planes, rows_here, pieces, block_len)
    local_part = jnp.einsum("kij,fqwkj->fqwki", down_maps, blocked, precision=HIGHEST_MODE)
    inflow = local_chain(enter_gain[:, -1], local_part[:, :, :, :, -1], 3, False)
    reduced = local_part + enter_gain[None, None, None, :, :] * inflow[:, :, :, :, None]
    swept = jnp.einsum("kij,fqwkj->fqwki", back_maps, reduced, precision=HIGHEST_MODE)
    outflow = local_chain(leave_gain[:, 0], swept[:, :, :, :, 0], 3, True)
    slopes = swept + leave_gain[None, None, None, :, :] * outflow[:, :, :, :, None]
    slopes = slopes.reshape(fields, planes, rows_here, length_all)
    return lax.all_to_all(slopes, "span", split_axis=3, concat_axis=1, tiled=True)


def per_device(conserved, wall_metric, span_metric):
    wall_part = wall_whole_lines(
        lax.all_to_all(conserved, "wall", split_axis=1, concat_axis=2, tiled=True)
    )
    span_part = span_whole_lines(
        lax.all_to_all(conserved, "span", split_axis=1, concat_axis=3, tiled=True)
    )
    return (wall_metric[None] * wall_part, span_metric[None] * span_part)


def solution(mesh):
    in_specs = (
        P(None, "stream", "wall", "span"),
        P("stream", "wall", "span"),
        P("stream", "wall", "span"),
    )
    out_specs = (P(None, "stream", "wall", "span"), P(None, "stream", "wall", "span"))
    return jax.shard_map(
        per_device, mesh=mesh, in_specs=in_specs, out_specs=out_specs, check_vma=False
    )
```

profile of v0, /device:TPU:0, one launch (start us, length us, event | category | flops | bytes accessed | tf_op | source)
XLA Modules:
  0.0 244.5 jit_solution(17826317619358397584)
XLA Ops:
  0.6 4.3 %copy.88 = f32[5,16,96,128]{3,2,0,1:T(8,128)} copy(f32[5,16,96,128]{3,2,1,0:T(8,128)} %param.13) | data formatting | bytes 7864320 | tf_op args[0]
  5.0 5.0 %all-to-all-start.2 = ((f32[5,16,96,128]{3,2,0,1:T(8,128)}), f32[5,16,96,128]{3,2,0,1:T(8,128)}, u32[]{:S(2)}, u32[]{:S(2)}) async-start(f32[5,16,96,128]{3,2,0,1:T(8,128)} %copy.88), calls=%async_computation.2 | async-start | bytes 7864320 | tf_op jit(solution)/shard_map/all_to_all | solution.py:141
  9.9 0.1 broadcast_in_dim.71
  10.1 0.1 broadcast_in_dim.80
  10.3 0.1 broadcast_in_dim.64
  10.3 0.1 broadcast_in_dim.76
  10.5 45.7 %all-to-all-done.2 = f32[5,16,96,128]{3,2,0,1:T(8,128)} async-done(((f32[5,16,96,128]{3,2,0,1:T(8,128)}), f32[5,16,96,128]{3,2,0,1:T(8,128)}, u32[]{:S(2)}, u32[]{:S(2)}) %all-to-all-start.2) | async-done | bytes 3932192 | tf_op jit(solution)/shard_map/all_to_all | solution.py:141
  56.1 8.3 %all-to-all-start = ((f32[5,16,96,128]{3,2,0,1:T(8,128)}), f32[5,16,96,128]{3,2,0,1:T(8,128)}, u32[]{:S(2)}, u32[]{:S(2)}) async-start(f32[5,16,96,128]{3,2,0,1:T(8,128)} %copy.88), calls=%async_computation | async-start | bytes 7864320 | tf_op jit(solution)/shard_map/all_to_all | solution.py:138
  64.5 6.9 %copy.133 = f32[5,4,4,96,128]{4,1,3,2,0:T(4,128)} copy(f32[5,4,4,96,128]{4,3,0,2,1:T(8,128)} %bitcast.19) | data formatting | bytes 7864320 | tf_op jit(solution)/shard_map/all_to_all | solution.py:141
  71.4 5.4 %all_to_all.51 = f32[5,4,96,512]{3,2,1,0:T(8,128)} reshape(f32[5,4,96,4,128]{4,3,2,1,0:T(4,128)} %bitcast.77) | data formatting | bytes 7864320 | tf_op jit(solution)/shard_map/all_to_all | solution.py:141
  76.8 11.5 %fusion.25 = f32[5,4,96,4,128]{4,2,1,0,3:T(8,128)S(1)} fusion(f32[4,128,128,1,1]{2,1,4,3,0:T(8,128)S(1)} %copy-done.25, f32[5,4,96,512]{3,2,1,0:T(8,128)} %all_to_all.51, f32[512]{0:T(512)S(1)} %copy-done.26, f32[512]{0:T(512)S(1)} %copy-done.27, f32[512]{0:T(512)S(1)} %copy-done.28, f32[512]{0:T(512)S(1)} %copy-done.29, f32[512]{0:T(512)S(1)} %copy-done.30), kind=kOutput, calls=%fused_computation.32 | convolution fusion | flops 1518796800 | bytes 8136704 | tf_op jit(solution)/shard_map/kij,fqwkj->fqwki/dot_general | solution.py:126
  88.4 1.9 copy-done.2
  90.3 3.0 %slice.570 = f32[5,4,96,4,1]{4,2,1,0,3:T(8,128)} slice(f32[5,4,96,4,128]{4,2,1,0,3:T(8,128)S(1)} %fusion.25), slice={[0:5], [0:4], [0:96], [0:4], [127:128]} | slice | bytes 61440 | tf_op jit(solution)/shard_map/slice | solution.py:127
  93.2 2.8 %copy.101 = f32[5,4,96,4,1]{2,3,1,0,4:T(4,128)S(1)} copy(f32[5,4,96,4,1]{4,2,1,0,3:T(8,128)} %slice.570) | data formatting | bytes 61440 | tf_op jit(solution)/shard_map/slice | solution.py:127
  96.0 0.1 slice.512
  96.2 0.1 slice.511
  96.3 0.1 multiply_add_fusion.4
  96.5 0.3 pad.138
  96.8 0.3 pad.244
  97.2 6.8 %fusion.22 = f32[5,4,96,4,128]{4,2,1,0,3:T(8,128)} fusion(f32[4,128,128,1,1]{2,1,4,3,0:T(8,128)S(1)} %copy-done.7, f32[5,4,96,4,128]{4,2,1,0,3:T(8,128)} %copy-done.2, f32[5,4,96,4]{2,1,0,3:T(4,128)S(1)} %concatenate.45.clone, f32[4,128]{1,0:T(4,128)S(1)} %copy-done.18), kind=kOutput, calls=%fused_computation.31 | convolution fusion | flops 1511915520 | bytes 8159232 | tf_op jit(solution)/shard_map/kij,fqwkj->fqwki/dot_general | solution.py:129
  104.0 2.8 %copy.103 = f32[5,4,96,4,1]{2,3,1,0,4:T(4,128)S(1)} copy(f32[5,4,96,4,1]{4,2,1,0,3:T(8,128)} %bitcast.73) | data formatting | bytes 61440 | tf_op jit(solution)/shard_map/slice | solution.py:130
  106.8 0.1 slice.530
  106.9 0.1 slice.528
  107.3 0.3 pad.140
  107.6 0.3 pad.245
  108.0 4.2 %multiply_add_fusion = f32[5,4,96,4,128]{4,2,1,0,3:T(8,128)} fusion(f32[5,4,96,4,128]{4,2,1,0,3:T(8,128)} %fusion.22, f32[5,4,96,4]{2,1,0,3:T(4,128)S(1)} %concatenate.47.clone, f32[4,128]{1,0:T(4,128)S(1)} %copy-done.15), kind=kLoop, calls=%fused_computation.21 | loop fusion | flops 1966080 | bytes 7897088 | tf_op jit(solution)/shard_map/add | solution.py:131
  112.2 6.7 %copy.113 = f32[5,4,96,4,128]{2,1,0,4,3:T(4,128)} copy(f32[5,4,96,4,128]{4,2,1,0,3:T(8,128)} %multiply_add_fusion) | data formatting | bytes 7864320 | tf_op jit(solution)/shard_map/reshape | solution.py:132
  118.9 5.1 %all-to-all-start.3 = ((f32[5,4,96,512]{2,1,0,3:T(4,128)}), f32[5,4,96,512]{2,1,0,3:T(4,128)}, u32[]{:S(2)}, u32[]{:S(2)}) async-start(f32[5,4,96,512]{2,1,0,3:T(4,128)} %bitcast.74), calls=%async_computation.3 | async-start | bytes 10485760 | tf_op jit(solution)/shard_map/all_to_all | solution.py:133
  124.1 2.5 %copy.89 = f32[5,16,96,128]{3,2,1,0:T(8,128)S(1)} copy(f32[5,16,96,128]{3,2,0,1:T(8,128)} %all-to-all-done) | data formatting | bytes 7864320 | tf_op jit(solution)/shard_map/all_to_all | solution.py:138
  126.6 2.6 %multiply_add_fusion.2 = f32[5,1,1536,128]{3,2,0,1:T(8,128)S(1)} fusion(f32[5,1,1536,128]{3,2,0,1:T(8,128)S(1)} %bitcast.76, f32[1536]{0:T(1024)S(1)} %copy-done.10, f32[1536]{0:T(1024)S(1)} %copy-done.11, f32[1536]{0:T(1024)S(1)} %copy-done.12, f32[1536]{0:T(1024)S(1)} %copy-done.13, f32[1536]{0:T(1024)S(1)} %copy-done.14), kind=kLoop, calls=%fused_computation.28 | loop fusion | flops 8847360 | bytes 7895040 | tf_op jit(solution)/shard_map/add | solution.py:80
  129.3 3.7 %fusion.28 = f32[5,1,16,96,128]{4,3,0,2,1:T(8,128)S(1)} fusion(f32[16,96,96,1]{2,1,3,0:T(8,128)S(1)} %copy-done.6, f32[5,16,96,128]{3,2,1,0:T(8,128)S(1)} %bitcast.75), kind=kOutput, calls=%fused_computation.33 | convolution fusion | flops 1132462080 | bytes 8454144 | tf_op jit(solution)/shard_map/kij,fqkjs->fqkis/dot_general | solution.py:108
  133.0 1.9 copy-done.1
  135.1 0.1 multiply_add_fusion.6
  135.2 0.1 multiply_add_fusion.8
  135.4 0.1 multiply_add_fusion.10
  135.8 0.1 fusion.39
  136.1 6.1 %fusion.31 = f32[5,1,16,96,128]{4,3,0,2,1:T(8,128)S(1)} fusion(f32[16,96,96,1]{2,1,3,0:T(8,128)S(1)} %copy-done.5, f32[5,1,16,96,128]{4,3,0,2,1:T(8,128)} %copy-done.1, f32[5,16,128]{2,0,1:T(8,128)S(1)} %copy.92, f32[16,96]{1,0:T(8,128)S(1)} %copy-done.9), kind=kOutput, calls=%fused_computation.34 | convolution fusion | flops 1134428160 | bytes 8501248 | tf_op jit(solution)/shard_map/kij,fqkjs->fqkis/dot_general | solution.py:111
  142.2 1.9 copy-done
  145.1 2.9 %multiply_add_fusion.1 = f32[5,1,16,96,128]{4,3,0,2,1:T(8,128)S(1)} fusion(f32[5,1,16,96,128]{4,3,0,2,1:T(8,128)} %copy-done, f32[5,16,128]{2,0,1:T(8,128)S(1)} %copy.94, f32[16,96]{1,0:T(8,128)S(1)} %copy-done.8), kind=kLoop, calls=%fused_computation.25 | loop fusion | flops 1966080 | bytes 7911424 | tf_op jit(solution)/shard_map/add | solution.py:113
  148.0 0.3 copy.95
  148.4 10.1 %copy.96 = f32[5,1,1536,128]{3,1,0,2:T(1,128)} copy(f32[5,1,1536,128]{3,2,0,1:T(8,128)S(1)} %bitcast.78) | data formatting | bytes 7864320 | tf_op jit(solution)/shard_map/reshape | solution.py:114
  158.4 24.8 %all-to-all-done.3 = f32[5,4,96,512]{2,1,0,3:T(4,128)} async-done(((f32[5,4,96,512]{2,1,0,3:T(4,128)}), f32[5,4,96,512]{2,1,0,3:T(4,128)}, u32[]{:S(2)}, u32[]{:S(2)}) %all-to-all-start.3) | async-done | bytes 3932192 | tf_op jit(solution)/shard_map/all_to_all | solution.py:133
  183.3 6.9 %all-to-all-start.1 = ((f32[5,1,1536,128]{3,1,0,2:T(1,128)}), f32[5,1,1536,128]{3,1,0,2:T(1,128)}, u32[]{:S(2)}, u32[]{:S(2)}) async-start(f32[5,1,1536,128]{3,1,0,2:T(1,128)} %copy.96), calls=%async_computation.1 | async-start | bytes 7864320 | tf_op jit(solution)/shard_map/all_to_all | solution.py:115
  190.2 6.8 %copy.108 = f32[5,4,4,96,128]{4,3,2,1,0:T(8,128)} copy(f32[5,4,4,96,128]{3,2,0,4,1:T(4,128)} %bitcast.32) | data formatting | bytes 7864320 | tf_op jit(solution)/shard_map/all_to_all | solution.py:133
  197.0 4.6 %broadcast_multiply_fusion = f32[5,16,96,128]{3,2,1,0:T(8,128)} fusion(f32[5,16,96,128]{3,2,1,0:T(8,128)} %bitcast.79, f32[16,96,128]{2,1,0:T(8,128)S(1)} %copy-done.3), kind=kLoop, calls=%fused_computation.37 | loop fusion | flops 983040 | bytes 8650752 | tf_op jit(solution)/shard_map/mul | solution.py:143
  201.6 38.0 %all-to-all-done.1 = f32[5,1,1536,128]{3,1,0,2:T(1,128)} async-done(((f32[5,1,1536,128]{3,1,0,2:T(1,128)}), f32[5,1,1536,128]{3,1,0,2:T(1,128)}, u32[]{:S(2)}, u32[]{:S(2)}) %all-to-all-start.1) | async-done | bytes 3932192 | tf_op jit(solution)/shard_map/all_to_all | solution.py:115
  239.6 2.4 copy.97
  242.0 2.5 %broadcast_multiply_fusion.1 = f32[5,16,96,128]{3,2,1,0:T(8,128)} fusion(f32[5,16,96,128]{3,2,1,0:T(8,128)S(1)} %bitcast.80, f32[16,96,128]{2,1,0:T(8,128)S(1)} %copy-done.4), kind=kLoop, calls=%fused_computation.40 | loop fusion | flops 983040 | bytes 8650752 | tf_op jit(solution)/shard_map/mul | solution.py:143
  (157 shorter events, 2.4 us)
Async XLA Ops:
  4.9 5.0 %copy-start.23 = (f32[7]{0:T(128)S(1)}, f32[7]{0:T(128)}, u32[]{:S(2)}) copy-start(f32[7]{0:T(128)} %constant.125) | copy-start | bytes 88
  4.9 5.1 %copy-start.24 = (f32[8]{0:T(128)S(1)}, f32[8]{0:T(128)}, u32[]{:S(2)}) copy-start(f32[8]{0:T(128)} %constant.126) | copy-start | bytes 100
  4.9 5.2 %copy-start.22 = (f32[2]{0:T(128)S(1)}, f32[2]{0:T(128)}, u32[]{:S(2)}) copy-start(f32[2]{0:T(128)} %constant.151) | copy-start | bytes 28
  4.9 5.3 %copy-start.16 = (f32[8]{0:T(128)S(1)}, f32[8]{0:T(128)}, u32[]{:S(2)}) copy-start(f32[8]{0:T(128)} %constant.109) | copy-start | bytes 100
  5.0 5.4 %copy-start.17 = (f32[2]{0:T(128)S(1)}, f32[2]{0:T(128)}, u32[]{:S(2)}) copy-start(f32[2]{0:T(128)} %constant.142) | copy-start | bytes 28
  5.0 51.2 %all-to-all-start.2 = ((f32[5,16,96,128]{3,2,0,1:T(8,128)}), f32[5,16,96,128]{3,2,0,1:T(8,128)}, u32[]{:S(2)}, u32[]{:S(2)}) async-start(f32[5,16,96,128]{3,2,0,1:T(8,128)} %copy.88), calls=%async_computation.2 | async-start | bytes 7864320 | tf_op jit(solution)/shard_map/all_to_all | solution.py:141
  56.1 62.8 %all-to-all-start = ((f32[5,16,96,128]{3,2,0,1:T(8,128)}), f32[5,16,96,128]{3,2,0,1:T(8,128)}, u32[]{:S(2)}, u32[]{:S(2)}) async-start(f32[5,16,96,128]{3,2,0,1:T(8,128)} %copy.88), calls=%async_computation | async-start | bytes 7864320 | tf_op jit(solution)/shard_map/all_to_all | solution.py:138
  71.4 5.4 %copy-start.25 = (f32[4,128,128,1,1]{2,1,4,3,0:T(8,128)S(1)}, f32[4,128,128,1,1]{2,1,4,3,0:T(8,128)}, u32[]{:S(2)}) copy-start(f32[4,128,128,1,1]{2,1,4,3,0:T(8,128)} %constant.156) | copy-start | bytes 786436
  71.4 5.4 %copy-start.26 = (f32[512]{0:T(512)S(1)}, f32[512]{0:T(512)}, u32[]{:S(2)}) copy-start(f32[512]{0:T(512)} %constant.137) | copy-start | bytes 6148
  71.4 5.4 %copy-start.27 = (f32[512]{0:T(512)S(1)}, f32[512]{0:T(512)}, u32[]{:S(2)}) copy-start(f32[512]{0:T(512)} %constant.135) | copy-start | bytes 6148
  71.4 5.4 %copy-start.28 = (f32[512]{0:T(512)S(1)}, f32[512]{0:T(512)}, u32[]{:S(2)}) copy-start(f32[512]{0:T(512)} %constant.133) | copy-start | bytes 6148
  71.4 5.4 %copy-start.29 = (f32[512]{0:T(512)S(1)}, f32[512]{0:T(512)}, u32[]{:S(2)}) copy-start(f32[512]{0:T(512)} %constant.131) | copy-start | bytes 6148
  71.4 5.4 %copy-start.30 = (f32[512]{0:T(512)S(1)}, f32[512]{0:T(512)}, u32[]{:S(2)}) copy-start(f32[512]{0:T(512)} %constant.129) | copy-start | bytes 6148
  88.4 1.9 copy-start.2
  93.2 3.9 %copy-start.7 = (f32[4,128,128,1,1]{2,1,4,3,0:T(8,128)S(1)}, f32[4,128,128,1,1]{2,1,4,3,0:T(8,128)}, u32[]{:S(2)}) copy-start(f32[4,128,128,1,1]{2,1,4,3,0:T(8,128)} %constant.157) | copy-start | bytes 786436
  93.2 3.9 %copy-start.18 = (f32[4,128]{1,0:T(4,128)S(1)}, f32[4,128]{1,0:T(4,128)}, u32[]{:S(2)}) copy-start(f32[4,128]{1,0:T(4,128)} %constant.33.clone) | copy-start | bytes 6148
  104.0 4.0 %copy-start.15 = (f32[4,128]{1,0:T(4,128)S(1)}, f32[4,128]{1,0:T(4,128)}, u32[]{:S(2)}) copy-start(f32[4,128]{1,0:T(4,128)} %constant.35.clone) | copy-start | bytes 6148
  118.9 64.3 %all-to-all-start.3 = ((f32[5,4,96,512]{2,1,0,3:T(4,128)}), f32[5,4,96,512]{2,1,0,3:T(4,128)}, u32[]{:S(2)}, u32[]{:S(2)}) async-start(f32[5,4,96,512]{2,1,0,3:T(4,128)} %bitcast.74), calls=%async_computation.3 | async-start | bytes 10485760 | tf_op jit(solution)/shard_map/all_to_all | solution.py:133
  124.0 2.5 %copy-start.10 = (f32[1536]{0:T(1024)S(1)}, f32[1536]{0:T(1024)}, u32[]{:S(2)}) copy-start(f32[1536]{0:T(1024)} %constant.105) | copy-start | bytes 18436
  124.0 2.5 %copy-start.11 = (f32[1536]{0:T(1024)S(1)}, f32[1536]{0:T(1024)}, u32[]{:S(2)}) copy-start(f32[1536]{0:T(1024)} %constant.103) | copy-start | bytes 18436
  124.0 2.5 %copy-start.12 = (f32[1536]{0:T(1024)S(1)}, f32[1536]{0:T(1024)}, u32[]{:S(2)}) copy-start(f32[1536]{0:T(1024)} %constant.101) | copy-start | bytes 18436
  124.1 2.5 %copy-start.13 = (f32[1536]{0:T(1024)S(1)}, f32[1536]{0:T(1024)}, u32[]{:S(2)}) copy-start(f32[1536]{0:T(1024)} %constant.99) | copy-start | bytes 18436
  124.1 2.5 %copy-start.14 = (f32[1536]{0:T(1024)S(1)}, f32[1536]{0:T(1024)}, u32[]{:S(2)}) copy-start(f32[1536]{0:T(1024)} %constant.97) | copy-start | bytes 18436
  126.6 2.7 %copy-start.6 = (f32[16,96,96,1]{2,1,3,0:T(8,128)S(1)}, f32[16,96,96,1]{2,1,3,0:T(8,128)}, u32[]{:S(2)}) copy-start(f32[16,96,96,1]{2,1,3,0:T(8,128)} %constant.154) | copy-start | bytes 1769476
  129.3 6.0 %copy-start.20 = (f32[4]{0:T(128)S(1)}, f32[4]{0:T(128)}, u32[]{:S(2)}) copy-start(f32[4]{0:T(128)} %constant.113) | copy-start | bytes 52
  129.3 6.1 %copy-start.21 = (f32[2]{0:T(128)S(1)}, f32[2]{0:T(128)}, u32[]{:S(2)}) copy-start(f32[2]{0:T(128)} %constant.118) | copy-start | bytes 28
  129.3 6.5 %copy-start.19 = (f32[7]{0:T(128)S(1)}, f32[7]{0:T(128)}, u32[]{:S(2)}) copy-start(f32[7]{0:T(128)} %constant.108) | copy-start | bytes 88
  129.3 6.7 %copy-start.5 = (f32[16,96,96,1]{2,1,3,0:T(8,128)S(1)}, f32[16,96,96,1]{2,1,3,0:T(8,128)}, u32[]{:S(2)}) copy-start(f32[16,96,96,1]{2,1,3,0:T(8,128)} %constant.155) | copy-start | bytes 1769476
  129.3 6.7 %copy-start.9 = (f32[16,96]{1,0:T(8,128)S(1)}, f32[16,96]{1,0:T(8,128)}, u32[]{:S(2)}) copy-start(f32[16,96]{1,0:T(8,128)} %constant.28.clone) | copy-start | bytes 18436
  133.0 1.9 copy-start.1
  136.1 9.1 %copy-start.8 = (f32[16,96]{1,0:T(8,128)S(1)}, f32[16,96]{1,0:T(8,128)}, u32[]{:S(2)}) copy-start(f32[16,96]{1,0:T(8,128)} %constant.30.clone) | copy-start | bytes 18436
  142.2 1.9 copy-start
  183.3 56.3 %all-to-all-start.1 = ((f32[5,1,1536,128]{3,1,0,2:T(1,128)}), f32[5,1,1536,128]{3,1,0,2:T(1,128)}, u32[]{:S(2)}, u32[]{:S(2)}) async-start(f32[5,1,1536,128]{3,1,0,2:T(1,128)} %copy.96), calls=%async_computation.1 | async-start | bytes 7864320 | tf_op jit(solution)/shard_map/all_to_all | solution.py:115
  190.2 6.8 %copy-start.3 = (f32[16,96,128]{2,1,0:T(8,128)S(1)}, f32[16,96,128]{2,1,0:T(8,128)}, u32[]{:S(2)}) copy-start(f32[16,96,128]{2,1,0:T(8,128)} %param.15) | copy-start | bytes 2359300
  201.6 40.3 %copy-start.4 = (f32[16,96,128]{2,1,0:T(8,128)S(1)}, f32[16,96,128]{2,1,0:T(8,128)}, u32[]{:S(2)}) copy-start(f32[16,96,128]{2,1,0:T(8,128)} %param.14) | copy-start | bytes 2359300
where the time goes:
time: 245 us; the launch traced here: 244 us
  waiting for transfers between devices  108 us (44%)
  local copies, waits for them, and re-layouts  63.3 us (26%)
  matrix products  28.1 us (11%)
  starting transfers between devices  25.3 us (10%)
  other arithmetic  17.8 us (7%)
    all_to_all x1, waiting for transfers between devices, per_device(): lax.all_to_all(conserved, 'span', split_axis=1, concat_axis=3, tiled=True)  45.7 us
    all_to_all x1, waiting for transfers between devices, wall_whole_lines(): lax.all_to_all(slopes, 'wall', split_axis=2, concat_axis=1, tiled=True)  38 us
    all_to_all x1, waiting for transfers between devices, span_whole_lines(): lax.all_to_all(slopes, 'span', split_axis=3, concat_axis=1, tiled=True)  24.8 us
    all_to_all x2, local copies, waits for them, and re-layouts, per_device(): lax.all_to_all(conserved, 'span', split_axis=1, concat_axis=3, tiled=True)  12.3 us
    dot_general x1, matrix products, span_whole_lines(): jnp.einsum('kij,fqwkj->fqwki', down_maps, blocked, precision=HIGHEST_MODE)  11.5 us
    unnamed x69, local copies, waits for them, and re-layouts  10.9 us
    reshape x1, local copies, waits for them, and re-layouts, wall_whole_lines(): slopes = slopes.reshape(fields, planes, length_all, columns)  10.1 us
    all_to_all x1, starting transfers between devices, per_device(): lax.all_to_all(conserved, 'wall', split_axis=1, concat_axis=2, tiled=True)  8.32 us
  transfers between devices with their start and end apart: 4, of which 3 were waited for; matrix products, arithmetic and copies ran while one was open for 36% of the time, Pallas kernels for 0%

commit v1 on v0

v1 whole, which is shorter than its diff:
```python
import functools

import jax
import jax.numpy as jnp
import numpy as np
from jax import lax
from jax.experimental import pallas as pl
from jax.experimental.pallas import tpu as pltpu
from jax.sharding import PartitionSpec as P

F32 = jnp.float32
BF16 = jnp.bfloat16
band_alpha = 0.4995
LANES = 128
VMEM_LIMIT = 16 * 2**20


def line_coefficients(length_all):
    lower_band = np.full(length_all, band_alpha)
    lower_band[1] = 0.25
    lower_band[length_all - 2] = 0.25
    lower_band[0] = 0.0
    lower_band[length_all - 1] = 0.0
    scales = np.zeros(length_all)
    pivots = np.zeros(length_all)
    previous = 0.0
    for row_idx in range(length_all):
        scales[row_idx] = 1.0 / (1.0 - lower_band[row_idx] * previous)
        pivots[row_idx] = lower_band[row_idx] * scales[row_idx]
        previous = pivots[row_idx]
    near_coef = (band_alpha + 2.0) / 3.0
    far_coef = (4.0 * band_alpha - 1.0) / 12.0
    weights = np.zeros((5, length_all))
    weights[:, :] = np.array([-far_coef, -near_coef, 0.0, near_coef, far_coef])[:, None]
    weights[:, 1] = [0.0, -0.75, 0.0, 0.75, 0.0]
    weights[:, length_all - 2] = [0.0, -0.75, 0.0, 0.75, 0.0]
    weights[:, 0] = [0.0, 0.0, -1.5, 2.0, -0.5]
    weights[:, length_all - 1] = [0.5, -2.0, 1.5, 0.0, 0.0]
    return (lower_band, scales, pivots, weights)


@functools.lru_cache(maxsize=None)
def line_tables(length_all, pieces):
    block = length_all // pieces
    lower_band, scales, pivots, weights = line_coefficients(length_all)

    def solve(rows):
        out = np.zeros_like(rows)
        running = np.zeros(rows.shape[1])
        for i in range(length_all):
            running = (rows[i] - lower_band[i] * running) * scales[i]
            out[i] = running
        running = np.zeros(rows.shape[1])
        for i in range(length_all - 1, -1, -1):
            running = out[i] - pivots[i] * running
            out[i] = running
        return out

    stencil = np.zeros((length_all, length_all))
    for k in range(5):
        for g in range(length_all):
            if 0 <= g + k - 2 < length_all:
                stencil[g, g + k - 2] = weights[k, g]
    whole = solve(stencil)
    unit = np.zeros((length_all, 2 * pieces))
    for k in range(pieces):
        unit[k * block, k] = 1.0
        unit[k * block + block - 1, pieces + k] = 1.0
    inverse = solve(unit)
    t = {
        "diag": np.zeros((pieces, block, block)),
        "enter": np.zeros((pieces, block)),
        "leave": np.zeros((pieces, block)),
        "right": np.zeros((pieces, block)),
        "left": np.zeros((pieces, block)),
        "first": np.zeros(pieces),
        "last": np.zeros(pieces),
        "pass_right": np.ones(pieces),
        "pass_left": np.ones(pieces),
    }
    for k in range(pieces):
        lo, hi = k * block, k * block + block
        t["diag"][k] = whole[lo:hi, lo:hi]
        t["enter"][k] = inverse[lo:hi, k] / inverse[lo, k]
        t["leave"][k] = inverse[lo:hi, pieces + k] / inverse[hi - 1, pieces + k]
        if k < pieces - 1:
            t["pass_right"][k] = inverse[hi, k] / inverse[lo, k]
        if k > 0:
            t["pass_left"][k] = inverse[lo - 1, pieces + k] / inverse[hi - 1, pieces + k]
    for k in range(pieces):
        lo, hi = k * block, k * block + block
        if k < pieces - 1:
            t["right"][k] = whole[hi + 1, lo:hi] / t["enter"][k + 1][1]
        if k > 0:
            t["left"][k] = whole[lo - 2, lo:hi] / t["leave"][k - 1][block - 2]
    for k in range(pieces):
        lo, hi = k * block, k * block + block
        if k > 0:
            t["first"][k] = whole[lo, lo - 1] - t["right"][k - 1][block - 1]
        if k < pieces - 1:
            t["last"][k] = whole[hi - 1, hi] - t["left"][k + 1][0]
    return t


def doubling_coefficients(t, pieces):
    rounds = pieces.bit_length() - 1
    right, left = t["pass_right"], t["pass_left"]
    coef = np.zeros((pieces, rounds, 8))
    for r in range(rounds):
        half = 1 << r
        for k in range(pieces):
            base = k // half * half
            inside = slice(base, base + half)
            if (k // half) % 2:
                other = slice(base - half, base)
                coef[k, r, :6] = [np.prod(right[base:k]), 0.0, 1.0, np.prod(right[inside]), np.prod(left[other]), 1.0]
            else:
                other = slice(base + half, base + 2 * half)
                coef[k, r, :6] = [0.0, np.prod(left[k + 1 : base + half]), np.prod(right[other]), 1.0, 1.0, np.prod(left[inside])]
    for k in range(pieces):
        if k > 0:
            coef[k, halo_round(k - 1), 6] = t["first"][k]
        if k < pieces - 1:
            coef[k, halo_round(k), 7] = t["last"][k]
    pick = np.array([[float(k >= pieces // 2), float(k < pieces // 2)] for k in range(pieces)])
    return np.concatenate([coef.reshape(pieces, -1), pick], axis=1)


def halo_round(k):
    if k % 2 == 0:
        return 0
    if k % 4 == 1:
        return 1
    return 2 if k % 8 == 3 else 3


def split_table(x):
    x = np.asarray(x, np.float32)
    high = x.astype(BF16)
    rest = x - high.astype(np.float32)
    mid = rest.astype(BF16)
    low = (rest - mid.astype(np.float32)).astype(BF16)
    return high, mid, low


def split_parts(x):
    high = x.astype(BF16)
    rest = x - high.astype(F32)
    mid = rest.astype(BF16)
    low = (rest - mid.astype(F32)).astype(BF16)
    return high, mid, low


def dot(a, b, dims):
    return lax.dot_general(a, b, (dims, ((), ())), preferred_element_type=F32)


COEF_ROWS = 40
STEP = 8


def table_loads(sources, targets, sems, wall_count):
    for j, (source, target) in enumerate(zip(sources, targets)):
        at = lax.axis_index("wall") if j < wall_count else lax.axis_index("span")
        yield pltpu.make_async_copy(source.at[at], target, sems.at[j])


def wall_moment_kernel(x_hbm, *refs):
    sources, targets = refs[:7], refs[7:14]
    x_ref, pay_ref, other_ref, x_sems, t_sems = refs[14:]
    fields, planes, rows, _ = x_ref.shape
    per = planes // STEP

    def x_copy(i):
        piece = (i // per, pl.ds(i % per * STEP, STEP))
        return pltpu.make_async_copy(x_hbm.at[piece], x_ref.at[piece], x_sems.at[i])

    loads = list(table_loads(sources, targets, t_sems, 3))
    loads[0].start()
    for i in range(fields * per):
        x_copy(i).start()
    for load in loads[1:]:
        load.start()
    loads[0].wait()
    even = lax.axis_index("wall") % 2 == 0
    table = targets[0][...]
    right, left = table[:, 0:1], table[:, 1:2]

    def chunk(i, carry):
        x_copy(i).wait()
        f, at = i // per, pl.ds(i % per * STEP, STEP)
        x = x_ref[f, at]
        pay_ref[0, f, at] = jnp.sum(x * right[None], axis=1)
        pay_ref[1, f, at] = jnp.sum(x * left[None], axis=1)
        first, last = x[:, 0, :], x[:, rows - 1, :]
        pay_ref[2, f, at] = jnp.where(even, last, first)
        other_ref[f, at] = jnp.where(even, first, last)
        return carry

    lax.fori_loop(0, fields * per, chunk, 0)
    for load in loads[1:]:
        load.wait()


def wall_merge_kernel(last, first_round, sent_ref, got_ref, extra_ref, *refs):
    if first_round:
        coef_ref, pay_ref, state_ref = refs
    else:
        old_ref, coef_ref, pay_ref, state_ref = refs
    coef = coef_ref[...]

    def c(j):
        return coef[j : j + 1, 0:1]

    base = 0 if first_round else (16 if last else 8)
    got_r, got_l, halo = got_ref[0], got_ref[1], got_ref[2]
    for j, value in enumerate((c(base) * got_r, c(base + 1) * got_l, c(base + 6) * halo, c(base + 7) * halo)):
        state_ref[j] = value if first_round else old_ref[j] + value
    own_r = c(base + 2) * sent_ref[0] + c(base + 3) * got_r
    own_l = c(base + 4) * sent_ref[1] + c(base + 5) * got_l
    if last:
        pay_ref[0] = c(32) * own_l + c(33) * own_r
        pay_ref[1] = extra_ref[...]
    else:
        pay_ref[0] = own_r
        pay_ref[1] = own_l
        pay_ref[2] = extra_ref[...]


def wall_local_kernel(x_ref, table_ref, out_ref):
    fields, planes, block, lanes = x_ref.shape
    per = planes // STEP
    table = table_ref[...]
    pad = table.shape[1] - block
    d_high, d_mid, d_low = table[:block], table[block : 2 * block], table[2 * block :]
    lhs = jnp.concatenate([jnp.concatenate([d_high, d_high], axis=1), jnp.concatenate([d_mid, d_mid], axis=1)], axis=0)
    lhs2 = jnp.concatenate([d_high, d_low], axis=1)

    def stacked(a, b):
        return jnp.concatenate([a, a[:pad], b, b[:pad]], axis=0)

    def chunk(i, carry):
        f, q = i // per, i % per * STEP
        flat = jnp.concatenate([x_ref[f, q + j] for j in range(STEP)], axis=1)
        high, mid, low = split_parts(flat)
        main = dot(lhs, stacked(high, mid), ((1,), (0,)))
        rest = dot(lhs2, stacked(low, high), ((1,), (0,)))
        total = main[:block] + (main[block:] + rest)
        for j in range(STEP):
            out_ref[f, q + j] = total[:, j * lanes : (j + 1) * lanes]
        return carry

    lax.fori_loop(0, fields * per, chunk, 0)


def store_loop(count, per, out_hbm, buffer, sems, compute):
    def copy(i, slot):
        return pltpu.make_async_copy(buffer.at[slot], out_hbm.at[i // per, pl.ds(i % per * STEP, STEP)], sems.at[slot])

    def chunk(i, carry):
        slot = i % 2

        @pl.when(i >= 2)
        def _():
            copy(i - 2, slot).wait()

        compute(i // per, pl.ds(i % per * STEP, STEP), i, buffer.at[slot])
        copy(i, slot).start()
        return carry

    lax.fori_loop(0, count, chunk, 0)
    copy(count - 2, count % 2).wait()
    copy(count - 1, (count - 1) % 2).wait()


def wall_final_kernel(local_ref, metric_ref, old_ref, got_ref, coef_ref, table_ref, out_hbm, buffer, sems):
    fields, planes, block, lanes = local_ref.shape
    per = planes // STEP
    coef = coef_ref[...]
    table = table_ref[...]
    enter, leave = table[:, 2:3], table[:, 3:4]
    top = lax.broadcasted_iota(jnp.int32, (1, 8, 1), 1) == 0
    bottom = lax.broadcasted_iota(jnp.int32, (1, 8, 1), 1) == 7

    def c(j):
        return coef[j : j + 1, 0:1]

    def compute(f, at, i, out):
        got, halo = got_ref[0, f, at], got_ref[1, f, at]
        m, n = old_ref[0, f, at] + c(24) * got, old_ref[1, f, at] + c(25) * got
        first, last = old_ref[2, f, at] + c(30) * halo, old_ref[3, f, at] + c(31) * halo
        for lo, hi in ((0, 8), (8, block - 8), (block - 8, block)):
            total = local_ref[f, at, lo:hi] + enter[None, lo:hi] * m[:, None, :] + leave[None, lo:hi] * n[:, None, :]
            if lo == 0:
                total = total + jnp.where(top, first[:, None, :], 0.0)
            if hi == block:
                total = total + jnp.where(bottom, last[:, None, :], 0.0)
            out[:, lo:hi] = metric_ref[at, lo:hi] * total

    store_loop(fields * per, per, out_hbm, buffer, sems, compute)


def span_moment_kernel(x_ref, table_ref, pay_ref, other_ref):
    fields, planes, rows, columns = x_ref.shape
    per = planes // STEP
    even = lax.axis_index("span") % 2 == 0
    table = table_ref[...]

    def chunk(i, carry):
        flat = x_ref[i // per, pl.ds(i % per * STEP, STEP)].reshape(STEP * rows, columns)
        high, mid, low = split_parts(flat)
        main = dot(table[:16], jnp.concatenate([high, mid], axis=1), ((1,), (1,)))
        rest = dot(table[16:], jnp.concatenate([low, high], axis=1), ((1,), (1,)))
        total = main[:8] + (main[8:] + rest[:8])
        first, last = total[2:3], total[3:4]
        at = pl.ds(pl.multiple_of(i * STEP * rows, 128), STEP * rows)
        pay_ref[0:2, at] = total[0:2]
        pay_ref[2:3, at] = jnp.where(even, last, first)
        other_ref[:, at] = jnp.where(even, first, last)
        return carry

    lax.fori_loop(0, fields * per, chunk, 0)


def span_merge_kernel(sent_ref, got_ref, other_ref, coef_ref, pay_ref, state_ref):
    coef = coef_ref[...]

    def c(j):
        return coef[j : j + 1, 0:1]

    got_r, got_l, halo = got_ref[0:1], got_ref[1:2], got_ref[2:3]
    for j, value in enumerate((c(0) * got_r, c(1) * got_l, c(6) * halo, c(7) * halo)):
        state_ref[j : j + 1] = value
    own_r = c(2) * sent_ref[0:1] + c(3) * got_r
    own_l = c(4) * sent_ref[1:2] + c(5) * got_l
    pay_ref[0:1] = c(16) * own_l + c(17) * own_r
    pay_ref[1:2] = other_ref[...]


def span_final_kernel(x_ref, metric_ref, old_ref, got_ref, coef_ref, table_ref, edge_ref, out_hbm, buffer, sems):
    fields, planes, rows, n = x_ref.shape
    per = planes // STEP
    coef = coef_ref[...]
    table = table_ref[...]
    d_high, d_low = table[:, :n], table[:, 2 * n :]
    weights = jnp.concatenate([table[:, : 2 * n], table[:, : 2 * n]], axis=0)
    weights2 = jnp.concatenate([d_high, d_low], axis=0)

    def c(j):
        return coef[j : j + 1, 0:1]

    def compute(f, at, i, out):
        flat = x_ref[f, at].reshape(STEP * rows, n)
        high, mid, low = split_parts(flat)
        main = dot(jnp.concatenate([high, mid], axis=1), weights, ((1,), (0,)))
        rest = dot(jnp.concatenate([low, high], axis=1), weights2, ((1,), (0,)))
        line = pl.ds(pl.multiple_of(i * STEP * rows, 128), STEP * rows)
        got, halo, old = got_ref[0:1, line], got_ref[1:2, line], old_ref[:, line]
        state = jnp.concatenate(
            [old[0:1] + c(8) * got, old[1:2] + c(9) * got, old[2:3] + c(14) * halo, old[3:4] + c(15) * halo]
            + [jnp.zeros((4, STEP * rows), F32)]
        )
        s_high = state.astype(BF16).astype(F32)
        s_rest = state - s_high
        s_mid = s_rest.astype(BF16).astype(F32)
        s_low = s_rest - s_mid
        parts = jnp.concatenate([s_high, s_high, s_mid, s_high, s_mid, s_low], axis=0).astype(BF16)
        edge = dot(parts, edge_ref[...], ((0,), (0,)))
        total = main[:, :n] + (main[:, n:] + (rest + edge))
        out[...] = metric_ref[at] * total.reshape(STEP, rows, n)

    store_loop(fields * per, per, out_hbm, buffer, sems, compute)


def per_device(conserved, wall_metric, span_metric):
    fields, planes, rows, columns = conserved.shape
    wall_pieces, span_pieces = lax.axis_size("wall"), lax.axis_size("span")
    wt = line_tables(rows * wall_pieces, wall_pieces)
    st = line_tables(columns * span_pieces, span_pieces)
    chunks = fields * planes // STEP
    lines = fields * planes * rows
    vmem = pl.BlockSpec(memory_space=pltpu.VMEM)
    hbm = pl.BlockSpec(memory_space=pltpu.HBM)

    def shape(*dims, dtype=F32):
        return jax.ShapeDtypeStruct(dims, dtype)

    def call(kernel, in_specs, out_specs, out_shape, micros, name, scratch=()):
        return pl.pallas_call(
            kernel,
            in_specs=in_specs,
            out_specs=out_specs,
            out_shape=out_shape,
            scratch_shapes=list(scratch),
            compiler_params=pltpu.CompilerParams(vmem_limit_bytes=VMEM_LIMIT),
            cost_estimate=pl.CostEstimate(flops=0, transcendentals=0, bytes_accessed=int(micros * 3.0e6)),
            name=name,
        )

    wall_rows = np.zeros((wall_pieces, rows, LANES), np.float32)
    for j, key in enumerate(("right", "left", "enter", "leave")):
        wall_rows[:, :, j] = wt[key]
    wall_diag = np.zeros((wall_pieces, 3 * rows, LANES), BF16)
    wall_diag[:, :, :rows] = np.concatenate(split_table(wt["diag"]), axis=1)
    span_diag = np.concatenate(split_table(np.swapaxes(st["diag"], 1, 2)), axis=2)
    pick = np.zeros((span_pieces, 4, columns))
    pick[:, 0], pick[:, 1] = st["right"], st["left"]
    pick[:, 2, 0] = 1.0
    pick[:, 3, columns - 1] = 1.0
    p_high, p_mid, p_low = split_table(pick)
    span_pick = np.zeros((span_pieces, 32, 2 * columns), BF16)
    span_pick[:, 0:4] = np.concatenate([p_high, p_high], axis=2)
    span_pick[:, 8:12] = np.concatenate([p_mid, p_mid], axis=2)
    span_pick[:, 16:20] = np.concatenate([p_high, p_low], axis=2)
    spread = np.zeros((span_pieces, 8, columns))
    spread[:, 0], spread[:, 1] = st["enter"], st["leave"]
    spread[:, 2, 0] = 1.0
    spread[:, 3, columns - 1] = 1.0
    e_high, e_mid, e_low = split_table(spread)
    span_edge = np.concatenate([e_high, e_mid, e_high, e_low, e_mid, e_high], axis=1)

    def spread_coefficients(t, pieces):
        c = doubling_coefficients(t, pieces)
        out = np.zeros((pieces, COEF_ROWS, LANES), np.float32)
        out[:, : c.shape[1]] = c[:, :, None]
        return out

    tables = [wall_rows, wall_diag, spread_coefficients(wt, wall_pieces)]
    tables += [span_diag, span_pick, span_edge, spread_coefficients(st, span_pieces)]
    tables = [pltpu.with_memory_space_constraint(jnp.asarray(t), pltpu.HBM) for t in tables]
    grid_values = pltpu.with_memory_space_constraint(conserved, pltpu.HBM)

    state = shape(4, fields, planes, columns)
    moment = shape(3, fields, planes, columns)
    out = call(
        wall_moment_kernel,
        [hbm] * 8,
        [vmem] * 10,
        [shape(*t.shape[1:], dtype=t.dtype) for t in tables]
        + [shape(*conserved.shape), moment, shape(fields, planes, columns)],
        2.5, "wall_moments",
        [pltpu.SemaphoreType.DMA((chunks,)), pltpu.SemaphoreType.DMA((len(tables),))],
    )(grid_values, *tables)
    w_rows, w_diag, w_coef, s_diag, s_pick, s_edge, s_coef, x, pay_w, other_w = out

    def swap(flip, pieces):
        return [(k, k ^ flip) for k in range(pieces)]

    got_w = lax.ppermute(pay_w, "wall", swap(1, wall_pieces))

    pay_s, other_s = call(
        span_moment_kernel, [vmem] * 2, [vmem] * 2, [shape(3, lines), shape(1, lines)], 3.4, "span_moments"
    )(x, s_pick)
    got_s = lax.ppermute(pay_s, "span", swap(1, span_pieces))

    pay_w, state_w = call(
        functools.partial(wall_merge_kernel, False, True), [vmem] * 4, [vmem] * 2, [moment, state], 0.2, "wall_merge_0"
    )(pay_w, got_w, other_w, w_coef)
    got_w = lax.ppermute(pay_w, "wall", swap(3, wall_pieces))
    halo = got_w[2]

    local_w = call(
        wall_local_kernel, [vmem] * 2, vmem, shape(*conserved.shape), 3.5, "wall_local"
    )(x, w_diag)

    pay_s, state_s = call(
        span_merge_kernel, [vmem] * 4, [vmem] * 2, [shape(2, lines), shape(4, lines)], 0.2, "span_merge"
    )(pay_s, got_s, other_s, s_coef)
    got_s = lax.ppermute(pay_s, "span", swap(3, span_pieces))

    pay_w, state_w = call(
        functools.partial(wall_merge_kernel, False, False), [vmem] * 5, [vmem] * 2, [moment, state], 0.2, "wall_merge_1"
    )(pay_w, got_w, halo, state_w, w_coef)
    got_w = lax.ppermute(pay_w, "wall", swap(4, wall_pieces))

    pay_w, state_w = call(
        functools.partial(wall_merge_kernel, True, False), [vmem] * 5, [vmem] * 2,
        [shape(2, fields, planes, columns), state], 0.2, "wall_merge_2",
    )(pay_w, got_w, halo, state_w, w_coef)
    got_w = lax.ppermute(pay_w, "wall", swap(12, wall_pieces))

    buffers = [pltpu.VMEM((2, STEP, rows, columns), F32), pltpu.SemaphoreType.DMA((2,))]
    span_slope = call(
        span_final_kernel, [vmem] * 7, hbm, shape(*conserved.shape), 6.0, "span_final", buffers
    )(x, span_metric, state_s, got_s, s_coef, s_diag, s_edge)
    wall_slope = call(
        wall_final_kernel, [vmem] * 6, hbm, shape(*conserved.shape), 4.0, "wall_final", buffers
    )(local_w, wall_metric, state_w, got_w, w_coef, w_rows)
    return (wall_slope, span_slope)


def solution(mesh):
    in_specs = (
        P(None, "stream", "wall", "span"),
        P("stream", "wall", "span"),
        P("stream", "wall", "span"),
    )
    out_specs = (P(None, "stream", "wall", "span"), P(None, "stream", "wall", "span"))
    return jax.shard_map(
        per_device, mesh=mesh, in_specs=in_specs, out_specs=out_specs, check_vma=False
    )
```

time: 245 us -> 44.5 us (0.18)
  waiting for transfers between devices: 108 us -> 7.24 us
  local copies, waits for them, and re-layouts: 63.3 us -> 0.01 us
  matrix products: 28.1 us -> 0 us
  Pallas kernels: 0 us -> 22 us
  other arithmetic: 17.8 us -> 0 us
  starting transfers between devices: 25.3 us -> 14.4 us
    all_to_all x4 -> x0, waiting for transfers between devices: 108 us -> none  [the longest x1 45.7 us: per_device(): lax.all_to_all(conserved, 'span', split_axis=1, concat_axis=3, tiled=True)]
    dot_general x4 -> x0, matrix products: 28.1 us -> none  [the longest x1 11.5 us: span_whole_lines(): jnp.einsum('kij,fqwkj->fqwki', down_maps, blocked, precision=HIGHEST_MODE)]
    all_to_all x4 -> x0, starting transfers between devices: 25.3 us -> none  [the longest x1 8.32 us: per_device(): lax.all_to_all(conserved, 'wall', split_axis=1, concat_axis=2, tiled=True)]
    all_to_all x5 -> x0, local copies, waits for them, and re-layouts: 23.9 us -> none  [the longest x2 12.3 us: per_device(): lax.all_to_all(conserved, 'span', split_axis=1, concat_axis=3, tiled=True)]
    pallas_call x0 -> x9, Pallas kernels: none -> 22 us  [the longest x1 7.05 us: per_device(): call(span_final_kernel, [vmem] * 7, hbm, shape(*conserved.shape), 6.0, 's...]
    reshape x2 -> x0, local copies, waits for them, and re-layouts: 16.7 us -> none  [the longest x1 10.1 us: wall_whole_lines(): slopes = slopes.reshape(fields, planes, length_all, columns)]
    ppermute x0 -> x6, starting transfers between devices: none -> 14.4 us  [the longest x1 3.94 us: per_device(): got_w = lax.ppermute(pay_w, 'wall', swap(3, wall_pieces))]
    unnamed x69 -> x4, local copies, waits for them, and re-layouts: 10.9 us -> 0.01 us
  transfers between devices with their start and end apart: 4 -> 6, of which waited for: 3 -> 3; matrix products, arithmetic and copies ran while one was open for 36% -> 0% of each run, Pallas kernels for 0% -> 32%
where the time goes in v1:
time: 44.5 us; the launch traced here: 44.4 us
  Pallas kernels  22 us (49%)
  starting transfers between devices  14.4 us (32%)
  waiting for transfers between devices  7.24 us (16%)
  between operations  0.73 us (2%)
    pallas_call x1, Pallas kernels, per_device(): call(span_final_kernel, [vmem] * 7, hbm, shape(*conserved.shape), 6.0, 's...  7.05 us
    pallas_call x1, Pallas kernels, per_device(): call(wall_final_kernel, [vmem] * 6, hbm, shape(*conserved.shape), 4.0, 'w...  4.7 us
    ppermute x1, starting transfers between devices, per_device(): got_w = lax.ppermute(pay_w, 'wall', swap(3, wall_pieces))  3.94 us
    pallas_call x1, Pallas kernels, per_device(): call(wall_local_kernel, [vmem] * 2, vmem, shape(*conserved.shape), 3.5, '...  3.46 us
    pallas_call x1, Pallas kernels, per_device(): call(span_moment_kernel, [vmem] * 2, [vmem] * 2, [shape(3, lines), shape(...  3.36 us
    ppermute x1, waiting for transfers between devices, per_device(): got_w = lax.ppermute(pay_w, 'wall', swap(1, wall_pieces))  3.32 us
    pallas_call x1, Pallas kernels, per_device(): call(wall_moment_kernel, [hbm] * 8, [vmem] * 10, [shape(*t.shape[1:], dty...  2.96 us
    ppermute x1, waiting for transfers between devices, per_device(): got_w = lax.ppermute(pay_w, 'wall', swap(3, wall_pieces))  2.86 us
  transfers between devices with their start and end apart: 6, of which 3 were waited for; matrix products, arithmetic and copies ran while one was open for 0% of the time, Pallas kernels for 32%

profile of v1, /device:TPU:0, one launch (start us, length us, event | category | flops | bytes accessed | tf_op | source)
XLA Modules:
  0.0 44.4 jit_solution(3074395976426308569)
XLA Ops:
  0.6 3.0 %wall_moments.1 = (f32[96,128]{1,0:T(8,128)S(1)}, bf16[288,128]{1,0:T(8,128)(2,1)S(1)}, f32[40,128]{1,0:T(8,128)S(1)}, bf16[128,384]{1,0:T(8,128)(2,1)S(1)}, bf1...) custom-call(f32[5,16,96,128]{3,2,1,0:T(8,128)} %x_hbm.1, ...), custom_call_target="tpu_custom_call" | custom-call | bytes 7500000 | tf_op jit(solution)/shard_map/wall_moments/pallas_call | solution.py:435
  3.6 2.1 %collective-permute-start = (f32[3,5,16,128]{3,2,1,0:T(8,128)S(1)}, f32[3,5,16,128]{3,2,1,0:T(8,128)S(1)}, u32[]{:S(2)}, u32[]{:S(2)}) collective-permute-start(f32[3,5,16,128]{3,2,1,0:T(8,128)S(1)} %get-tuple-element.24.sent_ref), channel_id=1, source_target_pairs={{0,8},{8,0},{16,24},{24,16},{32,40},{40,32},{48,56},{56,48},{64,72... | collective-permute-start | bytes 368648 | tf_op jit(solution)/shard_map/ppermute | solution.py:449
  5.7 3.3 %collective-permute-done.got_ref = f32[3,5,16,128]{3,2,1,0:T(8,128)S(1)} collective-permute-done((f32[3,5,16,128]{3,2,1,0:T(8,128)S(1)}, f32[3,5,16,128]{3,2,1,0:T(8,128)S(1)}, u32[]{:S(2)}, u32[]{:S(2)}) %collective-permute-start) | collective-permute-done | bytes 122912 | tf_op jit(solution)/shard_map/ppermute | solution.py:449
  9.0 0.1 wall_merge_0.1
  9.1 3.9 %collective-permute-start.1 = (f32[3,5,16,128]{3,2,1,0:T(8,128)S(1)}, f32[3,5,16,128]{3,2,1,0:T(8,128)S(1)}, u32[]{:S(2)}, u32[]{:S(2)}) collective-permute-start(f32[3,5,16,128]{3,2,1,0:T(8,128)S(1)} %get-tuple-element.27.sent_ref), channel_id=1, source_target_pairs={{0,24},{8,16},{16,8},{24,0},{32,56},{40,48},{48,40},{56,32},{64,88... | collective-permute-start | bytes 368648 | tf_op jit(solution)/shard_map/ppermute | solution.py:459
  13.0 2.9 %collective-permute-done.1.got_ref = f32[3,5,16,128]{3,2,1,0:T(8,128)S(1)} collective-permute-done((f32[3,5,16,128]{3,2,1,0:T(8,128)S(1)}, f32[3,5,16,128]{3,2,1,0:T(8,128)S(1)}, u32[]{:S(2)}, u32[]{:S(2)}) %collective-permute-start.1) | collective-permute-done | bytes 122912 | tf_op jit(solution)/shard_map/ppermute | solution.py:459
  15.9 0.1 wall_merge_1.1
  16.0 1.7 %collective-permute-start.2 = (f32[3,5,16,128]{3,2,1,0:T(8,128)S(1)}, f32[3,5,16,128]{3,2,1,0:T(8,128)S(1)}, u32[]{:S(2)}, u32[]{:S(2)}) collective-permute-start(f32[3,5,16,128]{3,2,1,0:T(8,128)S(1)} %get-tuple-element.29.sent_ref), channel_id=1, source_target_pairs={{0,32},{8,40},{16,48},{24,56},{32,0},{40,8},{48,16},{56,24},{64,96... | collective-permute-start | bytes 368648 | tf_op jit(solution)/shard_map/ppermute | solution.py:474
  17.6 3.4 %span_moments.1 = (f32[3,7680]{1,0:T(4,128)S(1)}, f32[1,7680]{1,0:T(1,128)S(1)}) custom-call(f32[5,16,96,128]{3,2,1,0:T(8,128)S(1)} %get-tuple-element.22.x_ref, bf16[32,256]{1,0:T(8,128)(2,1)S(1)} %get-tuple-element.34.table_ref), custom_call_target="tpu_custom_call" | custom-call | bytes 10200000 | tf_op jit(solution)/shard_map/span_moments/pallas_call | solution.py:451
  21.0 1.6 %collective-permute-start.4 = (f32[3,7680]{1,0:T(4,128)S(1)}, f32[3,7680]{1,0:T(4,128)S(1)}, u32[]{:S(2)}, u32[]{:S(2)}) collective-permute-start(f32[3,7680]{1,0:T(4,128)S(1)} %get-tuple-element.35.sent_ref), channel_id=1, source_target_pairs={{0,2},{2,0},{4,6},{6,4},{1,3},{3,1},{5,7},{7,5},{8,10},{10,8},{12,... | collective-permute-start | bytes 276488 | tf_op jit(solution)/shard_map/ppermute | solution.py:454
  22.6 0.0 collective-permute-done.2.got_ref
  22.6 0.1 wall_merge_2.1
  22.6 2.3 %collective-permute-start.3 = (f32[2,5,16,128]{3,2,1,0:T(8,128)S(1)}, f32[2,5,16,128]{3,2,1,0:T(8,128)S(1)}, u32[]{:S(2)}, u32[]{:S(2)}) collective-permute-start(f32[2,5,16,128]{3,2,1,0:T(8,128)S(1)} %get-tuple-element.32), channel_id=1, source_target_pairs={{0,96},{8,104},{16,112},{24,120},{32,64},{40,72},{48,80},{56,88},{... | collective-permute-start | bytes 245768 | tf_op jit(solution)/shard_map/ppermute | solution.py:480
  24.9 1.1 %collective-permute-done.4.got_ref = f32[3,7680]{1,0:T(4,128)S(1)} collective-permute-done((f32[3,7680]{1,0:T(4,128)S(1)}, f32[3,7680]{1,0:T(4,128)S(1)}, u32[]{:S(2)}, u32[]{:S(2)}) %collective-permute-start.4) | collective-permute-done | bytes 92192 | tf_op jit(solution)/shard_map/ppermute | solution.py:454
  26.0 0.3 span_merge.1
  26.3 2.8 %collective-permute-start.5 = (f32[2,7680]{1,0:T(2,128)S(1)}, f32[2,7680]{1,0:T(2,128)S(1)}, u32[]{:S(2)}, u32[]{:S(2)}) collective-permute-start(f32[2,7680]{1,0:T(2,128)S(1)} %get-tuple-element.39), channel_id=1, source_target_pairs={{0,6},{2,4},{4,2},{6,0},{1,7},{3,5},{5,3},{7,1},{8,14},{10,12},{12... | collective-permute-start | bytes 184328 | tf_op jit(solution)/shard_map/ppermute | solution.py:469
  29.1 0.0 copy-start
  29.1 3.5 %wall_local.1.local_ref = f32[5,16,96,128]{3,2,1,0:T(8,128)S(1)} custom-call(f32[5,16,96,128]{3,2,1,0:T(8,128)S(1)} %get-tuple-element.22.x_ref, bf16[288,128]{1,0:T(8,128)(2,1)S(1)} %get-tuple-element.23.table_ref), custom_call_target="tpu_custom_call" | custom-call | bytes 10500000 | tf_op jit(solution)/shard_map/wall_local/pallas_call | solution.py:462
  32.6 0.0 collective-permute-done.5.got_ref
  32.6 0.0 copy-done
  32.6 0.0 copy-start.1
  32.6 7.1 %span_final.1 = f32[5,16,96,128]{3,2,1,0:T(8,128)} custom-call(f32[5,16,96,128]{3,2,1,0:T(8,128)S(1)} %get-tuple-element.22.x_ref, f32[16,96,128]{2,1,0:T(8,128)S(1)} %copy-done, f32[4,7680]{1,0:T(4,128)S(1)} %get-tuple-element.38.old_ref, f32[2,7680]{1,0:T(2,128)S(1)} %collective-permute-done.5.got_ref, f32[40,128]{1,0:T(8,128)S(1)} %get-tuple-element.37.coef_ref, ...), custom_call_target="tpu_custom_call" | custom-call | bytes 18000000 | tf_op jit(solution)/shard_map/span_final/pallas_call | solution.py:483
  39.7 0.0 collective-permute-done.3.got_ref
  39.7 0.0 copy-done.1
  39.7 4.7 %wall_final.1 = f32[5,16,96,128]{3,2,1,0:T(8,128)} custom-call(f32[5,16,96,128]{3,2,1,0:T(8,128)S(1)} %wall_local.1.local_ref, f32[16,96,128]{2,1,0:T(8,128)S(1)} %copy-done.1, f32[4,5,16,128]{3,2,1,0:T(8,128)S(1)} %get-tuple-element.31.old_ref, f32[2,5,16,128]{3,2,1,0:T(8,128)S(1)} %collective-permute-done.3.got_ref, ...), custom_call_target="tpu_custom_call" | custom-call | bytes 12000000 | tf_op jit(solution)/shard_map/wall_final/pallas_call | solution.py:486
  (1 shorter events, 0.0 us)
Async XLA Ops:
  3.6 5.4 %collective-permute-start = (f32[3,5,16,128]{3,2,1,0:T(8,128)S(1)}, f32[3,5,16,128]{3,2,1,0:T(8,128)S(1)}, u32[]{:S(2)}, u32[]{:S(2)}) collective-permute-start(f32[3,5,16,128]{3,2,1,0:T(8,128)S(1)} %get-tuple-element.24.sent_ref), channel_id=1, source_target_pairs={{0,8},{8,0},{16,24},{24,16},{32,40},{40,32},{48,56},{56,48},{64,72... | collective-permute-start | bytes 368648 | tf_op jit(solution)/shard_map/ppermute | solution.py:449
  9.1 6.8 %collective-permute-start.1 = (f32[3,5,16,128]{3,2,1,0:T(8,128)S(1)}, f32[3,5,16,128]{3,2,1,0:T(8,128)S(1)}, u32[]{:S(2)}, u32[]{:S(2)}) collective-permute-start(f32[3,5,16,128]{3,2,1,0:T(8,128)S(1)} %get-tuple-element.27.sent_ref), channel_id=1, source_target_pairs={{0,24},{8,16},{16,8},{24,0},{32,56},{40,48},{48,40},{56,32},{64,88... | collective-permute-start | bytes 368648 | tf_op jit(solution)/shard_map/ppermute | solution.py:459
  16.0 6.6 %collective-permute-start.2 = (f32[3,5,16,128]{3,2,1,0:T(8,128)S(1)}, f32[3,5,16,128]{3,2,1,0:T(8,128)S(1)}, u32[]{:S(2)}, u32[]{:S(2)}) collective-permute-start(f32[3,5,16,128]{3,2,1,0:T(8,128)S(1)} %get-tuple-element.29.sent_ref), channel_id=1, source_target_pairs={{0,32},{8,40},{16,48},{24,56},{32,0},{40,8},{48,16},{56,24},{64,96... | collective-permute-start | bytes 368648 | tf_op jit(solution)/shard_map/ppermute | solution.py:474
  21.0 5.0 %collective-permute-start.4 = (f32[3,7680]{1,0:T(4,128)S(1)}, f32[3,7680]{1,0:T(4,128)S(1)}, u32[]{:S(2)}, u32[]{:S(2)}) collective-permute-start(f32[3,7680]{1,0:T(4,128)S(1)} %get-tuple-element.35.sent_ref), channel_id=1, source_target_pairs={{0,2},{2,0},{4,6},{6,4},{1,3},{3,1},{5,7},{7,5},{8,10},{10,8},{12,... | collective-permute-start | bytes 276488 | tf_op jit(solution)/shard_map/ppermute | solution.py:454
  22.6 17.0 %collective-permute-start.3 = (f32[2,5,16,128]{3,2,1,0:T(8,128)S(1)}, f32[2,5,16,128]{3,2,1,0:T(8,128)S(1)}, u32[]{:S(2)}, u32[]{:S(2)}) collective-permute-start(f32[2,5,16,128]{3,2,1,0:T(8,128)S(1)} %get-tuple-element.32), channel_id=1, source_target_pairs={{0,96},{8,104},{16,112},{24,120},{32,64},{40,72},{48,80},{56,88},{... | collective-permute-start | bytes 245768 | tf_op jit(solution)/shard_map/ppermute | solution.py:480
  26.3 6.3 %collective-permute-start.5 = (f32[2,7680]{1,0:T(2,128)S(1)}, f32[2,7680]{1,0:T(2,128)S(1)}, u32[]{:S(2)}, u32[]{:S(2)}) collective-permute-start(f32[2,7680]{1,0:T(2,128)S(1)} %get-tuple-element.39), channel_id=1, source_target_pairs={{0,6},{2,4},{4,2},{6,0},{1,7},{3,5},{5,3},{7,1},{8,14},{10,12},{12... | collective-permute-start | bytes 184328 | tf_op jit(solution)/shard_map/ppermute | solution.py:469
  29.1 3.5 %copy-start = (f32[16,96,128]{2,1,0:T(8,128)S(1)}, f32[16,96,128]{2,1,0:T(8,128)}, u32[]{:S(2)}) copy-start(f32[16,96,128]{2,1,0:T(8,128)} %metric_ref.3) | copy-start | bytes 2359300
  32.6 7.1 %copy-start.1 = (f32[16,96,128]{2,1,0:T(8,128)S(1)}, f32[16,96,128]{2,1,0:T(8,128)}, u32[]{:S(2)}) copy-start(f32[16,96,128]{2,1,0:T(8,128)} %metric_ref.2) | copy-start | bytes 2359300

commit v2 on v1

--- a/solution.py
+++ b/solution.py
@@ -8,11 +8,12 @@
 from jax.experimental.pallas import tpu as pltpu
 from jax.sharding import PartitionSpec as P
 
+
 F32 = jnp.float32
 BF16 = jnp.bfloat16
 band_alpha = 0.4995
 LANES = 128
-VMEM_LIMIT = 16 * 2**20
+VMEM_LIMIT = 24 * 2**20
 
 
 def line_coefficients(length_all):
@@ -155,7 +156,7 @@
     return lax.dot_general(a, b, (dims, ((), ())), preferred_element_type=F32)
 
 
-COEF_ROWS = 40
+SPAN_MOMENT_CHUNKS = 2
 STEP = 8
 
 
@@ -169,35 +170,28 @@
     sources, targets = refs[:7], refs[7:14]
     x_ref, pay_ref, other_ref, x_sems, t_sems = refs[14:]
     fields, planes, rows, _ = x_ref.shape
-    per = planes // STEP
-
-    def x_copy(i):
-        piece = (i // per, pl.ds(i % per * STEP, STEP))
-        return pltpu.make_async_copy(x_hbm.at[piece], x_ref.at[piece], x_sems.at[i])
 
     loads = list(table_loads(sources, targets, t_sems, 3))
+    copies = [pltpu.make_async_copy(x_hbm.at[f], x_ref.at[f], x_sems.at[f]) for f in range(fields)]
     loads[0].start()
-    for i in range(fields * per):
-        x_copy(i).start()
+    for copy in copies:
+        copy.start()
     for load in loads[1:]:
         load.start()
     loads[0].wait()
     even = lax.axis_index("wall") % 2 == 0
-    table = targets[0][...]
+    table = targets[0][...].T[:rows]
     right, left = table[:, 0:1], table[:, 1:2]
-
-    def chunk(i, carry):
-        x_copy(i).wait()
-        f, at = i // per, pl.ds(i % per * STEP, STEP)
-        x = x_ref[f, at]
-        pay_ref[0, f, at] = jnp.sum(x * right[None], axis=1)
-        pay_ref[1, f, at] = jnp.sum(x * left[None], axis=1)
-        first, last = x[:, 0, :], x[:, rows - 1, :]
-        pay_ref[2, f, at] = jnp.where(even, last, first)
-        other_ref[f, at] = jnp.where(even, first, last)
-        return carry
-
-    lax.fori_loop(0, fields * per, chunk, 0)
+    for f in range(fields):
+        copies[f].wait()
+        for q in range(0, planes, STEP):
+            at = slice(q, q + STEP)
+            x = x_ref[f, at]
+            pay_ref[0, f, at] = jnp.sum(x * right[None], axis=1)
+            pay_ref[1, f, at] = jnp.sum(x * left[None], axis=1)
+            first, last = x[:, 0, :], x[:, rows - 1, :]
+            pay_ref[2, f, at] = jnp.where(even, last, first)
+            other_ref[f, at] = jnp.where(even, first, last)
     for load in loads[1:]:
         load.wait()
 
@@ -210,7 +204,7 @@
     coef = coef_ref[...]
 
     def c(j):
-        return coef[j : j + 1, 0:1]
+        return coef[:, j : j + 1]
 
     base = 0 if first_round else (16 if last else 8)
     got_r, got_l, halo = got_ref[0], got_ref[1], got_ref[2]
@@ -229,7 +223,6 @@
 
 def wall_local_kernel(x_ref, table_ref, out_ref):
     fields, planes, block, lanes = x_ref.shape
-    per = planes // STEP
     table = table_ref[...]
     pad = table.shape[1] - block
     d_high, d_mid, d_low = table[:block], table[block : 2 * block], table[2 * block :]
@@ -239,94 +232,70 @@
     def stacked(a, b):
         return jnp.concatenate([a, a[:pad], b, b[:pad]], axis=0)
 
-    def chunk(i, carry):
-        f, q = i // per, i % per * STEP
-        flat = jnp.concatenate([x_ref[f, q + j] for j in range(STEP)], axis=1)
+    for f in range(fields):
+        flat = jnp.concatenate([x_ref[f, q] for q in range(planes)], axis=1)
         high, mid, low = split_parts(flat)
         main = dot(lhs, stacked(high, mid), ((1,), (0,)))
         rest = dot(lhs2, stacked(low, high), ((1,), (0,)))
         total = main[:block] + (main[block:] + rest)
-        for j in range(STEP):
-            out_ref[f, q + j] = total[:, j * lanes : (j + 1) * lanes]
-        return carry
-
-    lax.fori_loop(0, fields * per, chunk, 0)
-
-
-def store_loop(count, per, out_hbm, buffer, sems, compute):
-    def copy(i, slot):
-        return pltpu.make_async_copy(buffer.at[slot], out_hbm.at[i // per, pl.ds(i % per * STEP, STEP)], sems.at[slot])
-
-    def chunk(i, carry):
-        slot = i % 2
-
-        @pl.when(i >= 2)
-        def _():
-            copy(i - 2, slot).wait()
-
-        compute(i // per, pl.ds(i % per * STEP, STEP), i, buffer.at[slot])
-        copy(i, slot).start()
-        return carry
-
-    lax.fori_loop(0, count, chunk, 0)
-    copy(count - 2, count % 2).wait()
-    copy(count - 1, (count - 1) % 2).wait()
+        for q in range(planes):
+            out_ref[f, q] = total[:, q * lanes : (q + 1) * lanes]
 
 
 def wall_final_kernel(local_ref, metric_ref, old_ref, got_ref, coef_ref, table_ref, out_hbm, buffer, sems):
-    fields, planes, block, lanes = local_ref.shape
-    per = planes // STEP
+    fields, planes, block, _ = local_ref.shape
     coef = coef_ref[...]
-    table = table_ref[...]
+    table = table_ref[...].T[:block]
     enter, leave = table[:, 2:3], table[:, 3:4]
     top = lax.broadcasted_iota(jnp.int32, (1, 8, 1), 1) == 0
     bottom = lax.broadcasted_iota(jnp.int32, (1, 8, 1), 1) == 7
 
     def c(j):
-        return coef[j : j + 1, 0:1]
-
-    def compute(f, at, i, out):
-        got, halo = got_ref[0, f, at], got_ref[1, f, at]
-        m, n = old_ref[0, f, at] + c(24) * got, old_ref[1, f, at] + c(25) * got
-        first, last = old_ref[2, f, at] + c(30) * halo, old_ref[3, f, at] + c(31) * halo
-        for lo, hi in ((0, 8), (8, block - 8), (block - 8, block)):
-            total = local_ref[f, at, lo:hi] + enter[None, lo:hi] * m[:, None, :] + leave[None, lo:hi] * n[:, None, :]
-            if lo == 0:
-                total = total + jnp.where(top, first[:, None, :], 0.0)
-            if hi == block:
-                total = total + jnp.where(bottom, last[:, None, :], 0.0)
-            out[:, lo:hi] = metric_ref[at, lo:hi] * total
-
-    store_loop(fields * per, per, out_hbm, buffer, sems, compute)
+        return coef[:, j : j + 1]
+
+    copies = []
+    for f in range(fields):
+        for q in range(0, planes, STEP):
+            at = slice(q, q + STEP)
+            got, halo = got_ref[0, f, at], got_ref[1, f, at]
+            m, n = old_ref[0, f, at] + c(24) * got, old_ref[1, f, at] + c(25) * got
+            first, last = old_ref[2, f, at] + c(30) * halo, old_ref[3, f, at] + c(31) * halo
+            for lo, hi in ((0, 8), (8, block - 8), (block - 8, block)):
+                total = local_ref[f, at, lo:hi] + enter[None, lo:hi] * m[:, None, :] + leave[None, lo:hi] * n[:, None, :]
+                if lo == 0:
+                    total = total + jnp.where(top, first[:, None, :], 0.0)
+                if hi == block:
+                    total = total + jnp.where(bottom, last[:, None, :], 0.0)
+                buffer[f, at, lo:hi] = metric_ref[at, lo:hi] * total
+            copies.append(pltpu.make_async_copy(buffer.at[f, at], out_hbm.at[f, at], sems.at[len(copies)]))
+            copies[-1].start()
+    for copy in copies:
+        copy.wait()
 
 
 def span_moment_kernel(x_ref, table_ref, pay_ref, other_ref):
     fields, planes, rows, columns = x_ref.shape
-    per = planes // STEP
     even = lax.axis_index("span") % 2 == 0
     table = table_ref[...]
-
-    def chunk(i, carry):
-        flat = x_ref[i // per, pl.ds(i % per * STEP, STEP)].reshape(STEP * rows, columns)
+    for i in range(SPAN_MOMENT_CHUNKS):
+        lines = fields * planes * rows // SPAN_MOMENT_CHUNKS
+        at = slice(i * lines, (i + 1) * lines)
+        flat = x_ref[...].reshape(fields * planes * rows, columns)[at]
         high, mid, low = split_parts(flat)
         main = dot(table[:16], jnp.concatenate([high, mid], axis=1), ((1,), (1,)))
         rest = dot(table[16:], jnp.concatenate([low, high], axis=1), ((1,), (1,)))
         total = main[:8] + (main[8:] + rest[:8])
         first, last = total[2:3], total[3:4]
-        at = pl.ds(pl.multiple_of(i * STEP * rows, 128), STEP * rows)
         pay_ref[0:2, at] = total[0:2]
         pay_ref[2:3, at] = jnp.where(even, last, first)
         other_ref[:, at] = jnp.where(even, first, last)
-        return carry
-
-    lax.fori_loop(0, fields * per, chunk, 0)
 
 
 def span_merge_kernel(sent_ref, got_ref, other_ref, coef_ref, pay_ref, state_ref):
     coef = coef_ref[...]
 
     def c(j):
-        return coef[j : j + 1, 0:1]
+        return coef[:, j : j + 1]
 
     got_r, got_l, halo = got_ref[0:1], got_ref[1:2], got_ref[2:3]
     for j, value in enumerate((c(0) * got_r, c(1) * got_l, c(6) * halo, c(7) * halo)):
@@ -339,7 +308,6 @@
 
 def span_final_kernel(x_ref, metric_ref, old_ref, got_ref, coef_ref, table_ref, edge_ref, out_hbm, buffer, sems):
     fields, planes, rows, n = x_ref.shape
-    per = planes // STEP
     coef = coef_ref[...]
     table = table_ref[...]
     d_high, d_low = table[:, :n], table[:, 2 * n :]
@@ -347,18 +315,20 @@
     weights2 = jnp.concatenate([d_high, d_low], axis=0)
 
     def c(j):
-        return coef[j : j + 1, 0:1]
-
-    def compute(f, at, i, out):
-        flat = x_ref[f, at].reshape(STEP * rows, n)
+        return coef[:, j : j + 1]
+
+    copies = []
+    lines = planes * rows
+    for f in range(fields):
+        flat = x_ref[f].reshape(lines, n)
         high, mid, low = split_parts(flat)
         main = dot(jnp.concatenate([high, mid], axis=1), weights, ((1,), (0,)))
         rest = dot(jnp.concatenate([low, high], axis=1), weights2, ((1,), (0,)))
-        line = pl.ds(pl.multiple_of(i * STEP * rows, 128), STEP * rows)
+        line = slice(f * lines, (f + 1) * lines)
         got, halo, old = got_ref[0:1, line], got_ref[1:2, line], old_ref[:, line]
         state = jnp.concatenate(
             [old[0:1] + c(8) * got, old[1:2] + c(9) * got, old[2:3] + c(14) * halo, old[3:4] + c(15) * halo]
-            + [jnp.zeros((4, STEP * rows), F32)]
+            + [jnp.zeros((4, lines), F32)]
         )
         s_high = state.astype(BF16).astype(F32)
         s_rest = state - s_high
@@ -367,12 +337,14 @@
         parts = jnp.concatenate([s_high, s_high, s_mid, s_high, s_mid, s_low], axis=0).astype(BF16)
         edge = dot(parts, edge_ref[...], ((0,), (0,)))
         total = main[:, :n] + (main[:, n:] + (rest + edge))
-        out[...] = metric_ref[at] * total.reshape(STEP, rows, n)
-
-    store_loop(fields * per, per, out_hbm, buffer, sems, compute)
-
-
-def per_device(conserved, wall_metric, span_metric):
+        buffer[f] = metric_ref[...] * total.reshape(planes, rows, n)
+        copies.append(pltpu.make_async_copy(buffer.at[f], out_hbm.at[f], sems.at[f]))
+        copies[-1].start()
+    for copy in copies:
+        copy.wait()
+
+
+def slopes(conserved, wall_metric, span_metric):
     fields, planes, rows, columns = conserved.shape
     wall_pieces, span_pieces = lax.axis_size("wall"), lax.axis_size("span")
     wt = line_tables(rows * wall_pieces, wall_pieces)
@@ -385,7 +357,7 @@
     def shape(*dims, dtype=F32):
         return jax.ShapeDtypeStruct(dims, dtype)
 
-    def call(kernel, in_specs, out_specs, out_shape, micros, name, scratch=()):
+    def call(kernel, in_specs, out_specs, out_shape, micros, scratch=()):
         return pl.pallas_call(
             kernel,
             in_specs=in_specs,
@@ -394,12 +366,11 @@
             scratch_shapes=list(scratch),
             compiler_params=pltpu.CompilerParams(vmem_limit_bytes=VMEM_LIMIT),
             cost_estimate=pl.CostEstimate(flops=0, transcendentals=0, bytes_accessed=int(micros * 3.0e6)),
-            name=name,
         )
 
-    wall_rows = np.zeros((wall_pieces, rows, LANES), np.float32)
+    wall_rows = np.zeros((wall_pieces, 8, LANES), np.float32)
     for j, key in enumerate(("right", "left", "enter", "leave")):
-        wall_rows[:, :, j] = wt[key]
+        wall_rows[:, j, :rows] = wt[key]
     wall_diag = np.zeros((wall_pieces, 3 * rows, LANES), BF16)
     wall_diag[:, :, :rows] = np.concatenate(split_table(wt["diag"]), axis=1)
     span_diag = np.concatenate(split_table(np.swapaxes(st["diag"], 1, 2)), axis=2)
@@ -421,8 +392,8 @@
 
     def spread_coefficients(t, pieces):
         c = doubling_coefficients(t, pieces)
-        out = np.zeros((pieces, COEF_ROWS, LANES), np.float32)
-        out[:, : c.shape[1]] = c[:, :, None]
+        out = np.zeros((pieces, 1, LANES), np.float32)
+        out[:, 0, : c.shape[1]] = c
         return out
 
     tables = [wall_rows, wall_diag, spread_coefficients(wt, wall_pieces)]
@@ -438,8 +409,8 @@
         [vmem] * 10,
         [shape(*t.shape[1:], dtype=t.dtype) for t in tables]
         + [shape(*conserved.shape), moment, shape(fields, planes, columns)],
-        2.5, "wall_moments",
-        [pltpu.SemaphoreType.DMA((chunks,)), pltpu.SemaphoreType.DMA((len(tables),))],
+        2.5,
+        [pltpu.SemaphoreType.DMA((fields,)), pltpu.SemaphoreType.DMA((len(tables),))],
     )(grid_values, *tables)
     w_rows, w_diag, w_coef, s_diag, s_pick, s_edge, s_coef, x, pay_w, other_w = out
 
@@ -449,42 +420,39 @@
     got_w = lax.ppermute(pay_w, "wall", swap(1, wall_pieces))
 
     pay_s, other_s = call(
-        span_moment_kernel, [vmem] * 2, [vmem] * 2, [shape(3, lines), shape(1, lines)], 3.4, "span_moments"
+        span_moment_kernel, [vmem] * 2, [vmem] * 2, [shape(3, lines), shape(1, lines)], 3.4
     )(x, s_pick)
-    got_s = lax.ppermute(pay_s, "span", swap(1, span_pieces))
-
     pay_w, state_w = call(
-        functools.partial(wall_merge_kernel, False, True), [vmem] * 4, [vmem] * 2, [moment, state], 0.2, "wall_merge_0"
+        functools.partial(wall_merge_kernel, False, True), [vmem] * 4, [vmem] * 2, [moment, state], 0.2
     )(pay_w, got_w, other_w, w_coef)
     got_w = lax.ppermute(pay_w, "wall", swap(3, wall_pieces))
+    got_s = lax.ppermute(pay_s, "span", swap(1, span_pieces))
     halo = got_w[2]
 
-    local_w = call(
-        wall_local_kernel, [vmem] * 2, vmem, shape(*conserved.shape), 3.5, "wall_local"
-    )(x, w_diag)
+    local_w = call(wall_local_kernel, [vmem] * 2, vmem, shape(*conserved.shape), 3.5)(x, w_diag)
 
     pay_s, state_s = call(
-        span_merge_kernel, [vmem] * 4, [vmem] * 2, [shape(2, lines), shape(4, lines)], 0.2, "span_merge"
+        span_merge_kernel, [vmem] * 4, [vmem] * 2, [shape(2, lines), shape(4, lines)], 0.2
     )(pay_s, got_s, other_s, s_coef)
     got_s = lax.ppermute(pay_s, "span", swap(3, span_pieces))
 
     pay_w, state_w = call(
-        functools.partial(wall_merge_kernel, False, False), [vmem] * 5, [vmem] * 2, [moment, state], 0.2, "wall_merge_1"
+        functools.partial(wall_merge_kernel, False, False), [vmem] * 5, [vmem] * 2, [moment, state], 0.2
     )(pay_w, got_w, halo, state_w, w_coef)
     got_w = lax.ppermute(pay_w, "wall", swap(4, wall_pieces))
 
     pay_w, state_w = call(
         functools.partial(wall_merge_kernel, True, False), [vmem] * 5, [vmem] * 2,
-        [shape(2, fields, planes, columns), state], 0.2, "wall_merge_2",
+        [shape(2, fields, planes, columns), state], 0.2,
     )(pay_w, got_w, halo, state_w, w_coef)
     got_w = lax.ppermute(pay_w, "wall", swap(12, wall_pieces))
 
-    buffers = [pltpu.VMEM((2, STEP, rows, columns), F32), pltpu.SemaphoreType.DMA((2,))]
+    buffers = [pltpu.VMEM(conserved.shape, F32), pltpu.SemaphoreType.DMA((chunks,))]
     span_slope = call(
-        span_final_kernel, [vmem] * 7, hbm, shape(*conserved.shape), 6.0, "span_final", buffers
+        span_final_kernel, [vmem] * 7, hbm, shape(*conserved.shape), 6.0, buffers
     )(x, span_metric, state_s, got_s, s_coef, s_diag, s_edge)
     wall_slope = call(
-        wall_final_kernel, [vmem] * 6, hbm, shape(*conserved.shape), 4.0, "wall_final", buffers
+        wall_final_kernel, [vmem] * 6, hbm, shape(*conserved.shape), 4.0, buffers
     )(local_w, wall_metric, state_w, got_w, w_coef, w_rows)
     return (wall_slope, span_slope)
 
@@ -496,6 +464,4 @@
         P("stream", "wall", "span"),
     )
     out_specs = (P(None, "stream", "wall", "span"), P(None, "stream", "wall", "span"))
-    return jax.shard_map(
-        per_device, mesh=mesh, in_specs=in_specs, out_specs=out_specs, check_vma=False
-    )
+    return jax.shard_map(slopes, mesh=mesh, in_specs=in_specs, out_specs=out_specs, check_vma=False)

time: 44.5 us -> 36.7 us (0.82)
  Pallas kernels: 22 us -> 13.7 us
    pallas_call x9, Pallas kernels: 22 us -> 13.7 us  [the longest x1 4.12 us: slopes(): call(span_final_kernel, [vmem] * 7, hbm, shape(*conserved.shape), 6.0, bu...]
  transfers between devices with their start and end apart: 6 -> 6, of which waited for: 3 -> 4; matrix products, arithmetic and copies ran while one was open for 0% -> 0% of each run, Pallas kernels for 32% -> 24%
where the time goes in v2:
time: 36.7 us; the launch traced here: 36.5 us
  starting transfers between devices  14.7 us (40%)
  Pallas kernels  13.7 us (37%)
  waiting for transfers between devices  7.36 us (20%)
  between operations  0.7 us (2%)
    pallas_call x1, Pallas kernels, slopes(): call(span_final_kernel, [vmem] * 7, hbm, shape(*conserved.shape), 6.0, bu...  4.12 us
    ppermute x1, starting transfers between devices, slopes(): got_w = lax.ppermute(pay_w, 'wall', swap(3, wall_pieces))  3.94 us
    ppermute x1, waiting for transfers between devices, slopes(): got_w = lax.ppermute(pay_w, 'wall', swap(1, wall_pieces))  3.32 us
    ppermute x1, waiting for transfers between devices, slopes(): got_w = lax.ppermute(pay_w, 'wall', swap(3, wall_pieces))  2.86 us
    ppermute x1, starting transfers between devices, slopes(): got_s = lax.ppermute(pay_s, 'span', swap(3, span_pieces))  2.84 us
    ppermute x1, starting transfers between devices, slopes(): got_w = lax.ppermute(pay_w, 'wall', swap(12, wall_pieces))  2.63 us
    pallas_call x1, Pallas kernels, slopes(): call(wall_moment_kernel, [hbm] * 8, [vmem] * 10, [shape(*t.shape[1:], dty...  2.5 us
    pallas_call x1, Pallas kernels, slopes(): call(wall_final_kernel, [vmem] * 6, hbm, shape(*conserved.shape), 4.0, bu...  2.4 us
  transfers between devices with their start and end apart: 6, of which 4 were waited for; matrix products, arithmetic and copies ran while one was open for 0% of the time, Pallas kernels for 24%

profile of v2, /device:TPU:0, one launch (start us, length us, event | category | flops | bytes accessed | tf_op | source)
XLA Modules:
  0.0 36.5 jit_solution(16548001131444927324)
XLA Ops:
  0.6 2.5 %shard_map.113 = (f32[8,128]{1,0:T(8,128)S(1)}, bf16[288,128]{1,0:T(8,128)(2,1)S(1)}, f32[1,128]{1,0:T(1,128)S(1)}, bf16[128,384]{1,0:T(8,128)(2,1)S(1)}, bf16[3...) custom-call(f32[5,16,96,128]{3,2,1,0:T(8,128)} %x_hbm.1, ...), custom_call_target="tpu_custom_call" | custom-call | bytes 7500000 | tf_op jit(solution)/shard_map/pallas_call | solution.py:406
  3.1 2.1 %collective-permute-start = (f32[3,5,16,128]{3,2,1,0:T(8,128)S(1)}, f32[3,5,16,128]{3,2,1,0:T(8,128)S(1)}, u32[]{:S(2)}, u32[]{:S(2)}) collective-permute-start(f32[3,5,16,128]{3,2,1,0:T(8,128)S(1)} %get-tuple-element.24.sent_ref), channel_id=1, source_target_pairs={{0,8},{8,0},{16,24},{24,16},{32,40},{40,32},{48,56},{56,48},{64,72... | collective-permute-start | bytes 368648 | tf_op jit(solution)/shard_map/ppermute | solution.py:420
  5.2 3.3 %collective-permute-done.got_ref = f32[3,5,16,128]{3,2,1,0:T(8,128)S(1)} collective-permute-done((f32[3,5,16,128]{3,2,1,0:T(8,128)S(1)}, f32[3,5,16,128]{3,2,1,0:T(8,128)S(1)}, u32[]{:S(2)}, u32[]{:S(2)}) %collective-permute-start) | collective-permute-done | bytes 122912 | tf_op jit(solution)/shard_map/ppermute | solution.py:420
  8.6 0.1 shard_map.115
  8.7 3.9 %collective-permute-start.1 = (f32[3,5,16,128]{3,2,1,0:T(8,128)S(1)}, f32[3,5,16,128]{3,2,1,0:T(8,128)S(1)}, u32[]{:S(2)}, u32[]{:S(2)}) collective-permute-start(f32[3,5,16,128]{3,2,1,0:T(8,128)S(1)} %get-tuple-element.27.sent_ref), channel_id=1, source_target_pairs={{0,24},{8,16},{16,8},{24,0},{32,56},{40,48},{48,40},{56,32},{64,88... | collective-permute-start | bytes 368648 | tf_op jit(solution)/shard_map/ppermute | solution.py:428
  12.6 2.9 %collective-permute-done.1.got_ref = f32[3,5,16,128]{3,2,1,0:T(8,128)S(1)} collective-permute-done((f32[3,5,16,128]{3,2,1,0:T(8,128)S(1)}, f32[3,5,16,128]{3,2,1,0:T(8,128)S(1)}, u32[]{:S(2)}, u32[]{:S(2)}) %collective-permute-start.1) | collective-permute-done | bytes 122912 | tf_op jit(solution)/shard_map/ppermute | solution.py:428
  15.5 0.1 shard_map.116
  15.6 1.7 %collective-permute-start.2 = (f32[3,5,16,128]{3,2,1,0:T(8,128)S(1)}, f32[3,5,16,128]{3,2,1,0:T(8,128)S(1)}, u32[]{:S(2)}, u32[]{:S(2)}) collective-permute-start(f32[3,5,16,128]{3,2,1,0:T(8,128)S(1)} %get-tuple-element.29.sent_ref), channel_id=1, source_target_pairs={{0,32},{8,40},{16,48},{24,56},{32,0},{40,8},{48,16},{56,24},{64,96... | collective-permute-start | bytes 368648 | tf_op jit(solution)/shard_map/ppermute | solution.py:442
  17.2 2.2 %shard_map.119 = (f32[3,7680]{1,0:T(4,128)S(1)}, f32[1,7680]{1,0:T(1,128)S(1)}) custom-call(f32[5,16,96,128]{3,2,1,0:T(8,128)S(1)} %get-tuple-element.22.x_ref, bf16[32,256]{1,0:T(8,128)(2,1)S(1)} %get-tuple-element.34.table_ref), custom_call_target="tpu_custom_call" | custom-call | bytes 10200000 | tf_op jit(solution)/shard_map/pallas_call | solution.py:422
  19.4 1.6 %collective-permute-start.4 = (f32[3,7680]{1,0:T(4,128)S(1)}, f32[3,7680]{1,0:T(4,128)S(1)}, u32[]{:S(2)}, u32[]{:S(2)}) collective-permute-start(f32[3,7680]{1,0:T(4,128)S(1)} %get-tuple-element.35.sent_ref), channel_id=1, source_target_pairs={{0,2},{2,0},{4,6},{6,4},{1,3},{3,1},{5,7},{7,5},{8,10},{10,8},{12,... | collective-permute-start | bytes 276488 | tf_op jit(solution)/shard_map/ppermute | solution.py:429
  21.0 0.0 collective-permute-done.2.got_ref
  21.0 0.1 shard_map.117
  21.1 2.6 %collective-permute-start.3 = (f32[2,5,16,128]{3,2,1,0:T(8,128)S(1)}, f32[2,5,16,128]{3,2,1,0:T(8,128)S(1)}, u32[]{:S(2)}, u32[]{:S(2)}) collective-permute-start(f32[2,5,16,128]{3,2,1,0:T(8,128)S(1)} %get-tuple-element.32), channel_id=1, source_target_pairs={{0,96},{8,104},{16,112},{24,120},{32,64},{40,72},{48,80},{56,88},{... | collective-permute-start | bytes 245768 | tf_op jit(solution)/shard_map/ppermute | solution.py:448
  23.7 0.6 %collective-permute-done.4.got_ref = f32[3,7680]{1,0:T(4,128)S(1)} collective-permute-done((f32[3,7680]{1,0:T(4,128)S(1)}, f32[3,7680]{1,0:T(4,128)S(1)}, u32[]{:S(2)}, u32[]{:S(2)}) %collective-permute-start.4) | collective-permute-done | bytes 92192 | tf_op jit(solution)/shard_map/ppermute | solution.py:429
  24.4 0.1 shard_map.120
  24.5 2.8 %collective-permute-start.5 = (f32[2,7680]{1,0:T(2,128)S(1)}, f32[2,7680]{1,0:T(2,128)S(1)}, u32[]{:S(2)}, u32[]{:S(2)}) collective-permute-start(f32[2,7680]{1,0:T(2,128)S(1)} %get-tuple-element.39), channel_id=1, source_target_pairs={{0,6},{2,4},{4,2},{6,0},{1,7},{3,5},{5,3},{7,1},{8,14},{10,12},{12... | collective-permute-start | bytes 184328 | tf_op jit(solution)/shard_map/ppermute | solution.py:437
  27.3 0.0 copy-start
  27.3 2.1 %shard_map.114.local_ref = f32[5,16,96,128]{3,2,1,0:T(8,128)S(1)} custom-call(f32[5,16,96,128]{3,2,1,0:T(8,128)S(1)} %get-tuple-element.22.x_ref, bf16[288,128]{1,0:T(8,128)(2,1)S(1)} %get-tuple-element.23.table_ref), custom_call_target="tpu_custom_call" | custom-call | bytes 10500000 | tf_op jit(solution)/shard_map/pallas_call | solution.py:432
  29.4 0.5 %collective-permute-done.5.got_ref = f32[2,7680]{1,0:T(2,128)S(1)} collective-permute-done((f32[2,7680]{1,0:T(2,128)S(1)}, f32[2,7680]{1,0:T(2,128)S(1)}, u32[]{:S(2)}, u32[]{:S(2)}) %collective-permute-start.5) | collective-permute-done | bytes 61472 | tf_op jit(solution)/shard_map/ppermute | solution.py:437
  30.0 0.0 copy-done
  30.0 0.0 copy-start.1
  30.0 4.1 %shard_map.121 = f32[5,16,96,128]{3,2,1,0:T(8,128)} custom-call(f32[5,16,96,128]{3,2,1,0:T(8,128)S(1)} %get-tuple-element.22.x_ref, f32[16,96,128]{2,1,0:T(8,128)S(1)} %copy-done, f32[4,7680]{1,0:T(4,128)S(1)} %get-tuple-element.38.old_ref, f32[2,7680]{1,0:T(2,128)S(1)} %collective-permute-done.5.got_ref, f32[1,128]{1,0:T(1,128)S(1)} %get-tuple-element.37.coef_ref, ...), custom_call_target="tpu_custom_call" | custom-call | bytes 18000000 | tf_op jit(solution)/shard_map/pallas_call | solution.py:451
  34.1 0.0 collective-permute-done.3.got_ref
  34.1 0.0 copy-done.1
  34.1 2.4 %shard_map.118 = f32[5,16,96,128]{3,2,1,0:T(8,128)} custom-call(f32[5,16,96,128]{3,2,1,0:T(8,128)S(1)} %shard_map.114.local_ref, f32[16,96,128]{2,1,0:T(8,128)S(1)} %copy-done.1, f32[4,5,16,128]{3,2,1,0:T(8,128)S(1)} %get-tuple-element.31.old_ref, f32[2,5,16,128]{3,2,1,0:T(8,128)S(1)} %collective-permute-done.3.got_ref, ...), custom_call_target="tpu_custom_call" | custom-call | bytes 12000000 | tf_op jit(solution)/shard_map/pallas_call | solution.py:454
  (1 shorter events, 0.0 us)
Async XLA Ops:
  3.1 5.4 %collective-permute-start = (f32[3,5,16,128]{3,2,1,0:T(8,128)S(1)}, f32[3,5,16,128]{3,2,1,0:T(8,128)S(1)}, u32[]{:S(2)}, u32[]{:S(2)}) collective-permute-start(f32[3,5,16,128]{3,2,1,0:T(8,128)S(1)} %get-tuple-element.24.sent_ref), channel_id=1, source_target_pairs={{0,8},{8,0},{16,24},{24,16},{32,40},{40,32},{48,56},{56,48},{64,72... | collective-permute-start | bytes 368648 | tf_op jit(solution)/shard_map/ppermute | solution.py:420
  8.7 6.8 %collective-permute-start.1 = (f32[3,5,16,128]{3,2,1,0:T(8,128)S(1)}, f32[3,5,16,128]{3,2,1,0:T(8,128)S(1)}, u32[]{:S(2)}, u32[]{:S(2)}) collective-permute-start(f32[3,5,16,128]{3,2,1,0:T(8,128)S(1)} %get-tuple-element.27.sent_ref), channel_id=1, source_target_pairs={{0,24},{8,16},{16,8},{24,0},{32,56},{40,48},{48,40},{56,32},{64,88... | collective-permute-start | bytes 368648 | tf_op jit(solution)/shard_map/ppermute | solution.py:428
  15.6 5.4 %collective-permute-start.2 = (f32[3,5,16,128]{3,2,1,0:T(8,128)S(1)}, f32[3,5,16,128]{3,2,1,0:T(8,128)S(1)}, u32[]{:S(2)}, u32[]{:S(2)}) collective-permute-start(f32[3,5,16,128]{3,2,1,0:T(8,128)S(1)} %get-tuple-element.29.sent_ref), channel_id=1, source_target_pairs={{0,32},{8,40},{16,48},{24,56},{32,0},{40,8},{48,16},{56,24},{64,96... | collective-permute-start | bytes 368648 | tf_op jit(solution)/shard_map/ppermute | solution.py:442
  19.4 5.0 %collective-permute-start.4 = (f32[3,7680]{1,0:T(4,128)S(1)}, f32[3,7680]{1,0:T(4,128)S(1)}, u32[]{:S(2)}, u32[]{:S(2)}) collective-permute-start(f32[3,7680]{1,0:T(4,128)S(1)} %get-tuple-element.35.sent_ref), channel_id=1, source_target_pairs={{0,2},{2,0},{4,6},{6,4},{1,3},{3,1},{5,7},{7,5},{8,10},{10,8},{12,... | collective-permute-start | bytes 276488 | tf_op jit(solution)/shard_map/ppermute | solution.py:429
  21.1 13.0 %collective-permute-start.3 = (f32[2,5,16,128]{3,2,1,0:T(8,128)S(1)}, f32[2,5,16,128]{3,2,1,0:T(8,128)S(1)}, u32[]{:S(2)}, u32[]{:S(2)}) collective-permute-start(f32[2,5,16,128]{3,2,1,0:T(8,128)S(1)} %get-tuple-element.32), channel_id=1, source_target_pairs={{0,96},{8,104},{16,112},{24,120},{32,64},{40,72},{48,80},{56,88},{... | collective-permute-start | bytes 245768 | tf_op jit(solution)/shard_map/ppermute | solution.py:448
  24.5 5.5 %collective-permute-start.5 = (f32[2,7680]{1,0:T(2,128)S(1)}, f32[2,7680]{1,0:T(2,128)S(1)}, u32[]{:S(2)}, u32[]{:S(2)}) collective-permute-start(f32[2,7680]{1,0:T(2,128)S(1)} %get-tuple-element.39), channel_id=1, source_target_pairs={{0,6},{2,4},{4,2},{6,0},{1,7},{3,5},{5,3},{7,1},{8,14},{10,12},{12... | collective-permute-start | bytes 184328 | tf_op jit(solution)/shard_map/ppermute | solution.py:437
  27.3 2.7 %copy-start = (f32[16,96,128]{2,1,0:T(8,128)S(1)}, f32[16,96,128]{2,1,0:T(8,128)}, u32[]{:S(2)}) copy-start(f32[16,96,128]{2,1,0:T(8,128)} %metric_ref.3) | copy-start | bytes 2359300
  30.0 4.1 %copy-start.1 = (f32[16,96,128]{2,1,0:T(8,128)S(1)}, f32[16,96,128]{2,1,0:T(8,128)}, u32[]{:S(2)}) copy-start(f32[16,96,128]{2,1,0:T(8,128)} %metric_ref.2) | copy-start | bytes 2359300

commit v3 on v2

--- a/solution.py
+++ b/solution.py
@@ -156,7 +156,7 @@
     return lax.dot_general(a, b, (dims, ((), ())), preferred_element_type=F32)
 
 
-SPAN_MOMENT_CHUNKS = 2
+READY = ((0,), (1,))
 STEP = 8
 
 
@@ -172,7 +172,8 @@
     fields, planes, rows, _ = x_ref.shape
 
     loads = list(table_loads(sources, targets, t_sems, 3))
-    copies = [pltpu.make_async_copy(x_hbm.at[f], x_ref.at[f], x_sems.at[f]) for f in range(fields)]
+    pieces = [(f, slice(q, q + STEP)) for f in range(fields) for q in range(0, planes, STEP)]
+    copies = [pltpu.make_async_copy(x_hbm.at[p], x_ref.at[p], x_sems.at[i]) for i, p in enumerate(pieces)]
     loads[0].start()
     for copy in copies:
         copy.start()
@@ -182,16 +183,14 @@
     even = lax.axis_index("wall") % 2 == 0
     table = targets[0][...].T[:rows]
     right, left = table[:, 0:1], table[:, 1:2]
-    for f in range(fields):
-        copies[f].wait()
-        for q in range(0, planes, STEP):
-            at = slice(q, q + STEP)
-            x = x_ref[f, at]
-            pay_ref[0, f, at] = jnp.sum(x * right[None], axis=1)
-            pay_ref[1, f, at] = jnp.sum(x * left[None], axis=1)
-            first, last = x[:, 0, :], x[:, rows - 1, :]
-            pay_ref[2, f, at] = jnp.where(even, last, first)
-            other_ref[f, at] = jnp.where(even, first, last)
+    for copy, (f, at) in zip(copies, pieces):
+        copy.wait()
+        x = x_ref[f, at]
+        pay_ref[0, f, at] = jnp.sum(x * right[None], axis=1)
+        pay_ref[1, f, at] = jnp.sum(x * left[None], axis=1)
+        first, last = x[:, 0, :], x[:, rows - 1, :]
+        pay_ref[2, f, at] = jnp.where(even, last, first)
+        other_ref[f, at] = jnp.where(even, first, last)
     for load in loads[1:]:
         load.wait()
 
@@ -221,28 +220,38 @@
         pay_ref[2] = extra_ref[...]
 
 
-def wall_local_kernel(x_ref, table_ref, out_ref):
-    fields, planes, block, lanes = x_ref.shape
-    table = table_ref[...]
-    pad = table.shape[1] - block
-    d_high, d_mid, d_low = table[:block], table[block : 2 * block], table[2 * block :]
-    lhs = jnp.concatenate([jnp.concatenate([d_high, d_high], axis=1), jnp.concatenate([d_mid, d_mid], axis=1)], axis=0)
-    lhs2 = jnp.concatenate([d_high, d_low], axis=1)
-
-    def stacked(a, b):
-        return jnp.concatenate([a, a[:pad], b, b[:pad]], axis=0)
+def wall_local_kernel(high_ref, mid_ref, low_ref, table_ref, metric_a, metric_b, out_ref, metric_a_ref, metric_b_ref, sems):
+    fields, planes, block, lanes = out_ref.shape
+    loads = [pltpu.make_async_copy(metric_a, metric_a_ref, sems.at[0]), pltpu.make_async_copy(metric_b, metric_b_ref, sems.at[1])]
+    for load in loads:
+        load.start()
+    table = table_ref[...].astype(F32)
+    lane = lax.broadcasted_iota(jnp.int32, table.shape, 1)
+    again = pltpu.roll(table, block, 1)
+
+    def beside(a, b):
+        return jnp.concatenate([jnp.where(lane[:block] < block, a[0], b[1]), b[1]], axis=1)[:, : 2 * block].astype(BF16)
+
+    parts = [(table[j * block : (j + 1) * block], again[j * block : (j + 1) * block]) for j in range(3)]
+    lhs = jnp.concatenate([beside(parts[0], parts[0]), beside(parts[1], parts[1])], axis=0)
+    lhs2 = beside(parts[0], parts[2])
 
     for f in range(fields):
-        flat = jnp.concatenate([x_ref[f, q] for q in range(planes)], axis=1)
-        high, mid, low = split_parts(flat)
-        main = dot(lhs, stacked(high, mid), ((1,), (0,)))
-        rest = dot(lhs2, stacked(low, high), ((1,), (0,)))
+        high, mid, low = (
+            jnp.concatenate([ref[f, q] for q in range(planes)], axis=1) for ref in (high_ref, mid_ref, low_ref)
+        )
+        main = dot(lhs, jnp.concatenate([high, mid], axis=0), ((1,), (0,)))
+        rest = dot(lhs2, jnp.concatenate([low, high], axis=0), ((1,), (0,)))
         total = main[:block] + (main[block:] + rest)
         for q in range(planes):
             out_ref[f, q] = total[:, q * lanes : (q + 1) * lanes]
-
-
-def wall_final_kernel(local_ref, metric_ref, old_ref, got_ref, coef_ref, table_ref, out_hbm, buffer, sems):
+    for load in loads:
+        load.wait()
+
+
+def wall_final_kernel(
+    local_ref, metric_ref, old_ref, got_ref, coef_ref, table_ref, tail_ref, span_in, out_hbm, span_hbm, buffer, sems
+):
     fields, planes, block, _ = local_ref.shape
     coef = coef_ref[...]
     table = table_ref[...].T[:block]
@@ -253,7 +262,8 @@
     def c(j):
         return coef[:, j : j + 1]
 
-    copies = []
+    copies = [pltpu.make_async_copy(tail_ref, span_hbm.at[fields - 1], sems.at[0])]
+    copies[0].start()
     for f in range(fields):
         for q in range(0, planes, STEP):
             at = slice(q, q + STEP)
@@ -273,15 +283,16 @@
         copy.wait()
 
 
-def span_moment_kernel(x_ref, table_ref, pay_ref, other_ref):
+def span_moment_kernel(x_ref, table_ref, pay_ref, other_ref, high_ref, mid_ref, low_ref):
     fields, planes, rows, columns = x_ref.shape
     even = lax.axis_index("span") % 2 == 0
     table = table_ref[...]
-    for i in range(SPAN_MOMENT_CHUNKS):
-        lines = fields * planes * rows // SPAN_MOMENT_CHUNKS
-        at = slice(i * lines, (i + 1) * lines)
-        flat = x_ref[...].reshape(fields * planes * rows, columns)[at]
-        high, mid, low = split_parts(flat)
+    lines = planes * rows
+    for f in range(fields):
+        at = slice(f * lines, (f + 1) * lines)
+        high, mid, low = split_parts(x_ref[f].reshape(lines, columns))
+        for ref, part in ((high_ref, high), (mid_ref, mid), (low_ref, low)):
+            ref[f] = part.reshape(planes, rows, columns)
         main = dot(table[:16], jnp.concatenate([high, mid], axis=1), ((1,), (1,)))
         rest = dot(table[16:], jnp.concatenate([low, high], axis=1), ((1,), (1,)))
         total = main[:8] + (main[8:] + rest[:8])
@@ -291,6 +302,30 @@
         other_ref[:, at] = jnp.where(even, first, last)
 
 
+def span_matrices(table):
+    n = table.shape[0]
+    return (
+        jnp.concatenate([table[:, : 2 * n], table[:, : 2 * n]], axis=0),
+        jnp.concatenate([table[:, :n], table[:, 2 * n :]], axis=0),
+    )
+
+
+def span_product(weights, high, mid, low):
+    n = high.shape[1]
+    main = dot(jnp.concatenate([high, mid], axis=1), weights[0], ((1,), (0,)))
+    rest = dot(jnp.concatenate([low, high], axis=1), weights[1], ((1,), (0,)))
+    return main[:, :n], main[:, n:] + rest
+
+
+def span_local_kernel(start, high_ref, mid_ref, low_ref, table_ref, out_ref):
+    count, planes, rows, n = out_ref.shape
+    weights = span_matrices(table_ref[...])
+    for j in range(count):
+        parts = (ref[start + j].reshape(planes * rows, n) for ref in (high_ref, mid_ref, low_ref))
+        a, b = span_product(weights, *parts)
+        out_ref[j] = (a + b).reshape(planes, rows, n)
+
+
 def span_merge_kernel(sent_ref, got_ref, other_ref, coef_ref, pay_ref, state_ref):
     coef = coef_ref[...]
 
@@ -306,24 +341,20 @@
     pay_ref[1:2] = other_ref[...]
 
 
-def span_final_kernel(x_ref, metric_ref, old_ref, got_ref, coef_ref, table_ref, edge_ref, out_hbm, buffer, sems):
-    fields, planes, rows, n = x_ref.shape
+def span_final_kernel(ready, high_ref, mid_ref, low_ref, metric_ref, old_ref, got_ref, coef_ref, table_ref, edge_ref, *refs):
+    locals_ref = refs[: len(ready)]
+    out_hbm, tail_ref, buffer, sems = refs[len(ready) :]
+    fields, planes, rows, n = high_ref.shape
     coef = coef_ref[...]
-    table = table_ref[...]
-    d_high, d_low = table[:, :n], table[:, 2 * n :]
-    weights = jnp.concatenate([table[:, : 2 * n], table[:, : 2 * n]], axis=0)
-    weights2 = jnp.concatenate([d_high, d_low], axis=0)
+    weights = span_matrices(table_ref[...])
 
     def c(j):
         return coef[:, j : j + 1]
 
     copies = []
     lines = planes * rows
+    own = {f: (ref, j) for ref, group in zip(locals_ref, ready) for j, f in enumerate(group)}
     for f in range(fields):
-        flat = x_ref[f].reshape(lines, n)
-        high, mid, low = split_parts(flat)
-        main = dot(jnp.concatenate([high, mid], axis=1), weights, ((1,), (0,)))
-        rest = dot(jnp.concatenate([low, high], axis=1), weights2, ((1,), (0,)))
         line = slice(f * lines, (f + 1) * lines)
         got, halo, old = got_ref[0:1, line], got_ref[1:2, line], old_ref[:, line]
         state = jnp.concatenate(
@@ -336,10 +367,19 @@
         s_low = s_rest - s_mid
         parts = jnp.concatenate([s_high, s_high, s_mid, s_high, s_mid, s_low], axis=0).astype(BF16)
         edge = dot(parts, edge_ref[...], ((0,), (0,)))
-        total = main[:, :n] + (main[:, n:] + (rest + edge))
-        buffer[f] = metric_ref[...] * total.reshape(planes, rows, n)
-        copies.append(pltpu.make_async_copy(buffer.at[f], out_hbm.at[f], sems.at[f]))
-        copies[-1].start()
+        if f in own:
+            ref, j = own[f]
+            total = ref[j].reshape(lines, n) + edge
+        else:
+            a, b = span_product(weights, *(ref[f].reshape(lines, n) for ref in (high_ref, mid_ref, low_ref)))
+            total = a + (b + edge)
+        total = metric_ref[...] * total.reshape(planes, rows, n)
+        if f == fields - 1:
+            tail_ref[...] = total
+        else:
+            buffer[f] = total
+            copies.append(pltpu.make_async_copy(buffer.at[f], out_hbm.at[f], sems.at[f]))
+            copies[-1].start()
     for copy in copies:
         copy.wait()
 
@@ -357,13 +397,14 @@
     def shape(*dims, dtype=F32):
         return jax.ShapeDtypeStruct(dims, dtype)
 
-    def call(kernel, in_specs, out_specs, out_shape, micros, scratch=()):
+    def call(kernel, in_specs, out_specs, out_shape, micros, scratch=(), aliases=None):
         return pl.pallas_call(
             kernel,
             in_specs=in_specs,
             out_specs=out_specs,
             out_shape=out_shape,
             scratch_shapes=list(scratch),
+            input_output_aliases=aliases or {},
             compiler_params=pltpu.CompilerParams(vmem_limit_bytes=VMEM_LIMIT),
             cost_estimate=pl.CostEstimate(flops=0, transcendentals=0, bytes_accessed=int(micros * 3.0e6)),
         )
@@ -410,7 +451,7 @@
         [shape(*t.shape[1:], dtype=t.dtype) for t in tables]
         + [shape(*conserved.shape), moment, shape(fields, planes, columns)],
         2.5,
-        [pltpu.SemaphoreType.DMA((fields,)), pltpu.SemaphoreType.DMA((len(tables),))],
+        [pltpu.SemaphoreType.DMA((chunks,)), pltpu.SemaphoreType.DMA((len(tables),))],
     )(grid_values, *tables)
     w_rows, w_diag, w_coef, s_diag, s_pick, s_edge, s_coef, x, pay_w, other_w = out
 
@@ -419,17 +460,31 @@
 
     got_w = lax.ppermute(pay_w, "wall", swap(1, wall_pieces))
 
-    pay_s, other_s = call(
-        span_moment_kernel, [vmem] * 2, [vmem] * 2, [shape(3, lines), shape(1, lines)], 3.4
+    part = shape(*conserved.shape, dtype=BF16)
+    pay_s, other_s, *parts = call(
+        span_moment_kernel, [vmem] * 2, [vmem] * 5, [shape(3, lines), shape(1, lines)] + [part] * 3, 2.1
     )(x, s_pick)
+    got_s = lax.ppermute(pay_s, "span", swap(1, span_pieces))
+
     pay_w, state_w = call(
         functools.partial(wall_merge_kernel, False, True), [vmem] * 4, [vmem] * 2, [moment, state], 0.2
     )(pay_w, got_w, other_w, w_coef)
     got_w = lax.ppermute(pay_w, "wall", swap(3, wall_pieces))
-    got_s = lax.ppermute(pay_s, "span", swap(1, span_pieces))
     halo = got_w[2]
 
-    local_w = call(wall_local_kernel, [vmem] * 2, vmem, shape(*conserved.shape), 3.5)(x, w_diag)
+    local_w, span_metric, wall_metric = call(
+        wall_local_kernel, [vmem] * 4 + [hbm] * 2, [vmem] * 3,
+        [shape(*conserved.shape)] + [shape(*wall_metric.shape)] * 2, 1.7,
+        [pltpu.SemaphoreType.DMA((2,))],
+    )(*parts, w_diag, *(pltpu.with_memory_space_constraint(m, pltpu.HBM) for m in (span_metric, wall_metric)))
+
+    def span_local(group):
+        return call(
+            functools.partial(span_local_kernel, group[0]), [vmem] * 4, vmem,
+            shape(len(group), planes, rows, columns), 0.6 * len(group),
+        )(*parts, s_diag)
+
+    own_s = [span_local(group) for group in READY]
 
     pay_s, state_s = call(
         span_merge_kernel, [vmem] * 4, [vmem] * 2, [shape(2, lines), shape(4, lines)], 0.2
@@ -447,13 +502,15 @@
     )(pay_w, got_w, halo, state_w, w_coef)
     got_w = lax.ppermute(pay_w, "wall", swap(12, wall_pieces))
 
-    buffers = [pltpu.VMEM(conserved.shape, F32), pltpu.SemaphoreType.DMA((chunks,))]
-    span_slope = call(
-        span_final_kernel, [vmem] * 7, hbm, shape(*conserved.shape), 6.0, buffers
-    )(x, span_metric, state_s, got_s, s_coef, s_diag, s_edge)
-    wall_slope = call(
-        wall_final_kernel, [vmem] * 6, hbm, shape(*conserved.shape), 4.0, buffers
-    )(local_w, wall_metric, state_w, got_w, w_coef, w_rows)
+    span_slope, tail = call(
+        functools.partial(span_final_kernel, READY), [vmem] * (9 + len(READY)), [hbm, vmem],
+        [shape(*conserved.shape), shape(planes, rows, columns)], 3.0,
+        [pltpu.VMEM((fields - 1, planes, rows, columns), F32), pltpu.SemaphoreType.DMA((fields,))],
+    )(*parts, span_metric, state_s, got_s, s_coef, s_diag, s_edge, *own_s)
+    wall_slope, span_slope = call(
+        wall_final_kernel, [vmem] * 7 + [hbm], [hbm] * 2, [shape(*conserved.shape)] * 2, 2.4,
+        [pltpu.VMEM(conserved.shape, F32), pltpu.SemaphoreType.DMA((chunks + 1,))], {7: 1},
+    )(local_w, wall_metric, state_w, got_w, w_coef, w_rows, tail, span_slope)
     return (wall_slope, span_slope)
 
 

time: 36.7 us -> 35.6 us (0.970)
  Pallas kernels: 13.7 us -> 13.1 us
  waiting for transfers between devices: 7.36 us -> 6.98 us
    pallas_call x4 -> x6, Pallas kernels: 10.8 us -> 10.3 us  [the longest x1 2.72 us: slopes(): call(functools.partial(span_final_kernel, READY), [vmem] * (9 + len(READY...]
    ppermute x1, waiting for transfers between devices: 0.53 us -> 0.01 us  [slopes(): got_s = lax.ppermute(pay_s, 'span', swap(3, span_pieces))]
  transfers between devices with their start and end apart: 6 -> 6, of which waited for: 4 -> 3; matrix products, arithmetic and copies ran while one was open for 0% -> 0% of each run, Pallas kernels for 24% -> 23%
where the time goes in v3:
time: 35.6 us; the launch traced here: 35.5 us
  starting transfers between devices  14.7 us (41%)
  Pallas kernels  13.1 us (37%)
  waiting for transfers between devices  6.98 us (20%)
  between operations  0.72 us (2%)
    ppermute x1, starting transfers between devices, slopes(): got_w = lax.ppermute(pay_w, 'wall', swap(3, wall_pieces))  3.96 us
    ppermute x1, waiting for transfers between devices, slopes(): got_w = lax.ppermute(pay_w, 'wall', swap(1, wall_pieces))  3.32 us
    ppermute x1, waiting for transfers between devices, slopes(): got_w = lax.ppermute(pay_w, 'wall', swap(3, wall_pieces))  2.86 us
    ppermute x1, starting transfers between devices, slopes(): got_s = lax.ppermute(pay_s, 'span', swap(3, span_pieces))  2.84 us
    pallas_call x1, Pallas kernels, slopes(): call(functools.partial(span_final_kernel, READY), [vmem] * (9 + len(READY...  2.72 us
    ppermute x1, starting transfers between devices, slopes(): got_w = lax.ppermute(pay_w, 'wall', swap(12, wall_pieces))  2.49 us
    pallas_call x1, Pallas kernels, slopes(): call(wall_moment_kernel, [hbm] * 8, [vmem] * 10, [shape(*t.shape[1:], dty...  2.48 us
    pallas_call x1, Pallas kernels, slopes(): call(wall_final_kernel, [vmem] * 7 + [hbm], [hbm] * 2, [shape(*conserved....  2.42 us
  transfers between devices with their start and end apart: 6, of which 3 were waited for; matrix products, arithmetic and copies ran while one was open for 0% of the time, Pallas kernels for 23%

profile of v3, /device:TPU:0, one launch (start us, length us, event | category | flops | bytes accessed | tf_op | source)
XLA Modules:
  0.0 35.5 jit_solution(9052882776782945678)
XLA Ops:
  0.6 2.5 %shard_map.113 = (f32[8,128]{1,0:T(8,128)S(1)}, bf16[288,128]{1,0:T(8,128)(2,1)S(1)}, f32[1,128]{1,0:T(1,128)S(1)}, bf16[128,384]{1,0:T(8,128)(2,1)S(1)}, bf16[3...) custom-call(f32[5,16,96,128]{3,2,1,0:T(8,128)} %x_hbm.1, ...), custom_call_target="tpu_custom_call" | custom-call | bytes 7500000 | tf_op jit(solution)/shard_map/pallas_call | solution.py:447
  3.1 2.1 %collective-permute-start = (f32[3,5,16,128]{3,2,1,0:T(8,128)S(1)}, f32[3,5,16,128]{3,2,1,0:T(8,128)S(1)}, u32[]{:S(2)}, u32[]{:S(2)}) collective-permute-start(f32[3,5,16,128]{3,2,1,0:T(8,128)S(1)} %get-tuple-element.38.sent_ref), channel_id=1, source_target_pairs={{0,8},{8,0},{16,24},{24,16},{32,40},{40,32},{48,56},{56,48},{64,72... | collective-permute-start | bytes 368648 | tf_op jit(solution)/shard_map/ppermute | solution.py:461
  5.2 3.3 %collective-permute-done.got_ref = f32[3,5,16,128]{3,2,1,0:T(8,128)S(1)} collective-permute-done((f32[3,5,16,128]{3,2,1,0:T(8,128)S(1)}, f32[3,5,16,128]{3,2,1,0:T(8,128)S(1)}, u32[]{:S(2)}, u32[]{:S(2)}) %collective-permute-start) | collective-permute-done | bytes 122912 | tf_op jit(solution)/shard_map/ppermute | solution.py:461
  8.5 0.1 shard_map.116
  8.6 4.0 %collective-permute-start.1 = (f32[3,5,16,128]{3,2,1,0:T(8,128)S(1)}, f32[3,5,16,128]{3,2,1,0:T(8,128)S(1)}, u32[]{:S(2)}, u32[]{:S(2)}) collective-permute-start(f32[3,5,16,128]{3,2,1,0:T(8,128)S(1)} %get-tuple-element.41.sent_ref), channel_id=1, source_target_pairs={{0,24},{8,16},{16,8},{24,0},{32,56},{40,48},{48,40},{56,32},{64,88... | collective-permute-start | bytes 368648 | tf_op jit(solution)/shard_map/ppermute | solution.py:472
  12.6 2.9 %collective-permute-done.1.got_ref = f32[3,5,16,128]{3,2,1,0:T(8,128)S(1)} collective-permute-done((f32[3,5,16,128]{3,2,1,0:T(8,128)S(1)}, f32[3,5,16,128]{3,2,1,0:T(8,128)S(1)}, u32[]{:S(2)}, u32[]{:S(2)}) %collective-permute-start.1) | collective-permute-done | bytes 122912 | tf_op jit(solution)/shard_map/ppermute | solution.py:472
  15.4 0.1 shard_map.117
  15.5 1.7 %collective-permute-start.2 = (f32[3,5,16,128]{3,2,1,0:T(8,128)S(1)}, f32[3,5,16,128]{3,2,1,0:T(8,128)S(1)}, u32[]{:S(2)}, u32[]{:S(2)}) collective-permute-start(f32[3,5,16,128]{3,2,1,0:T(8,128)S(1)} %get-tuple-element.43.sent_ref), channel_id=1, source_target_pairs={{0,32},{8,40},{16,48},{24,56},{32,0},{40,8},{48,16},{56,24},{64,96... | collective-permute-start | bytes 368648 | tf_op jit(solution)/shard_map/ppermute | solution.py:497
  17.2 2.2 %shard_map.114 = (f32[3,7680]{1,0:T(4,128)S(1)}, f32[1,7680]{1,0:T(1,128)S(1)}, bf16[5,16,96,128]{3,2,1,0:T(8,128)(2,1)S(1)}, bf16[5,16,96,128]{3,2,1,0:T(8,128)(2,1)S(1)}, bf16[5,16,96,128]{3,2,1,0:T(8,128)(2,1)S(1)}) custom-call(f32[5,16,96,128]{3,2,1,0:T(8,128)S(1)} %get-tuple-element.30.x_ref, bf16[32,256]{1,0:T(8,128)(2,1)S(1)} %get-tuple-element.31.table_ref), custom_call_target="tpu_custom_call" | custom-call | bytes 6300000 | tf_op jit(solution)/shard_map/pallas_call | solution.py:464
  19.5 1.6 %collective-permute-start.4 = (f32[3,7680]{1,0:T(4,128)S(1)}, f32[3,7680]{1,0:T(4,128)S(1)}, u32[]{:S(2)}, u32[]{:S(2)}) collective-permute-start(f32[3,7680]{1,0:T(4,128)S(1)} %get-tuple-element.49.sent_ref), channel_id=1, source_target_pairs={{0,2},{2,0},{4,6},{6,4},{1,3},{3,1},{5,7},{7,5},{8,10},{10,8},{12,... | collective-permute-start | bytes 276488 | tf_op jit(solution)/shard_map/ppermute | solution.py:467
  21.0 0.0 collective-permute-done.2.got_ref
  21.0 0.1 shard_map.118
  21.1 2.5 %collective-permute-start.3 = (f32[2,5,16,128]{3,2,1,0:T(8,128)S(1)}, f32[2,5,16,128]{3,2,1,0:T(8,128)S(1)}, u32[]{:S(2)}, u32[]{:S(2)}) collective-permute-start(f32[2,5,16,128]{3,2,1,0:T(8,128)S(1)} %get-tuple-element.46), channel_id=1, source_target_pairs={{0,96},{8,104},{16,112},{24,120},{32,64},{40,72},{48,80},{56,88},{... | collective-permute-start | bytes 245768 | tf_op jit(solution)/shard_map/ppermute | solution.py:503
  23.6 0.8 %collective-permute-done.4.got_ref = f32[3,7680]{1,0:T(4,128)S(1)} collective-permute-done((f32[3,7680]{1,0:T(4,128)S(1)}, f32[3,7680]{1,0:T(4,128)S(1)}, u32[]{:S(2)}, u32[]{:S(2)}) %collective-permute-start.4) | collective-permute-done | bytes 92192 | tf_op jit(solution)/shard_map/ppermute | solution.py:467
  24.4 0.1 shard_map.119
  24.5 2.8 %collective-permute-start.5 = (f32[2,7680]{1,0:T(2,128)S(1)}, f32[2,7680]{1,0:T(2,128)S(1)}, u32[]{:S(2)}, u32[]{:S(2)}) collective-permute-start(f32[2,7680]{1,0:T(2,128)S(1)} %get-tuple-element.53), channel_id=1, source_target_pairs={{0,6},{2,4},{4,2},{6,0},{1,7},{3,5},{5,3},{7,1},{8,14},{10,12},{12... | collective-permute-start | bytes 184328 | tf_op jit(solution)/shard_map/ppermute | solution.py:492
  27.4 0.6 %shard_map.121.refs_1_ = f32[1,16,96,128]{3,2,1,0:T(8,128)S(1)} custom-call(bf16[5,16,96,128]{3,2,1,0:T(8,128)(2,1)S(1)} %get-tuple-element.32.high_ref, bf16[5,16,96,128]{3,2,1,0:T(8,128)(2,1)S(1)} %get-tuple-element.33.mid_ref, bf16[5,16,96,128]{3,2,1,0:T(8,128)(2,1)S(1)} %get-tuple-element.34.low_ref, bf16[128,384]{1,0:T(8,128)(2,1)S(1)} %get-tuple-element.54.table_ref), custom_call_target="tpu_custom_call" | custom-call | bytes 1800000 | tf_op jit(solution)/shard_map/pallas_call | solution.py:482
  27.9 0.6 %shard_map.120.refs_0_ = f32[1,16,96,128]{3,2,1,0:T(8,128)S(1)} custom-call(bf16[5,16,96,128]{3,2,1,0:T(8,128)(2,1)S(1)} %get-tuple-element.32.high_ref, bf16[5,16,96,128]{3,2,1,0:T(8,128)(2,1)S(1)} %get-tuple-element.33.mid_ref, bf16[5,16,96,128]{3,2,1,0:T(8,128)(2,1)S(1)} %get-tuple-element.34.low_ref, bf16[128,384]{1,0:T(8,128)(2,1)S(1)} %get-tuple-element.54.table_ref), custom_call_target="tpu_custom_call" | custom-call | bytes 1800000 | tf_op jit(solution)/shard_map/pallas_call | solution.py:482
  28.5 1.7 %shard_map.115 = (f32[5,16,96,128]{3,2,1,0:T(8,128)S(1)}, f32[16,96,128]{2,1,0:T(8,128)S(1)}, f32[16,96,128]{2,1,0:T(8,128)S(1)}) custom-call(bf16[5,16,96,128]{3,2,1,0:T(8,128)(2,1)S(1)} %get-tuple-element.32.high_ref, bf16[5,16,96,128]{3,2,1,0:T(8,128)(2,1)S(1)} %get-tuple-element.33.mid_ref, bf16[5,16,96,128]{3,2,1,0:T(8,128)(2,1)S(1)} %get-tuple-element.34.low_ref, ...), custom_call_target="tpu_custom_call" | custom-call | bytes 5100000 | tf_op jit(solution)/shard_map/pallas_call | solution.py:475
  30.3 0.0 collective-permute-done.5.got_ref
  30.3 2.7 %shard_map.122 = (f32[5,16,96,128]{3,2,1,0:T(8,128)}, f32[16,96,128]{2,1,0:T(8,128)S(1)}) custom-call(bf16[5,16,96,128]{3,2,1,0:T(8,128)(2,1)S(1)} %get-tuple-element.32.high_ref, bf16[5,16,96,128]{3,2,1,0:T(8,128)(2,1)S(1)} %get-tuple-element.33.mid_ref, bf16[5,16,96,128]{3,2,1,0:T(8,128)(2,1)S(1)} %get-tuple-element.34.low_ref, ...), custom_call_target="tpu_custom_call" | custom-call | bytes 9000000 | tf_op jit(solution)/shard_map/pallas_call | solution.py:505
  33.0 0.0 collective-permute-done.3.got_ref
  33.0 2.4 %shard_map.123 = (f32[5,16,96,128]{3,2,1,0:T(8,128)}, f32[5,16,96,128]{3,2,1,0:T(8,128)}) custom-call(f32[5,16,96,128]{3,2,1,0:T(8,128)S(1)} %get-tuple-element.36.local_ref, f32[16,96,128]{2,1,0:T(8,128)S(1)} %get-tuple-element.37.metric_ref, f32[4,5,16,128]{3,2,1,0:T(8,128)S(1)} %get-tuple-element.45.old_ref, ...), custom_call_target="tpu_custom_call", output_to_operand_aliasing={{1}: (7, {})} | custom-call | bytes 7200000 | tf_op jit(solution)/shard_map/pallas_call | solution.py:510
  (1 shorter events, 0.0 us)
Async XLA Ops:
  3.1 5.4 %collective-permute-start = (f32[3,5,16,128]{3,2,1,0:T(8,128)S(1)}, f32[3,5,16,128]{3,2,1,0:T(8,128)S(1)}, u32[]{:S(2)}, u32[]{:S(2)}) collective-permute-start(f32[3,5,16,128]{3,2,1,0:T(8,128)S(1)} %get-tuple-element.38.sent_ref), channel_id=1, source_target_pairs={{0,8},{8,0},{16,24},{24,16},{32,40},{40,32},{48,56},{56,48},{64,72... | collective-permute-start | bytes 368648 | tf_op jit(solution)/shard_map/ppermute | solution.py:461
  8.6 6.8 %collective-permute-start.1 = (f32[3,5,16,128]{3,2,1,0:T(8,128)S(1)}, f32[3,5,16,128]{3,2,1,0:T(8,128)S(1)}, u32[]{:S(2)}, u32[]{:S(2)}) collective-permute-start(f32[3,5,16,128]{3,2,1,0:T(8,128)S(1)} %get-tuple-element.41.sent_ref), channel_id=1, source_target_pairs={{0,24},{8,16},{16,8},{24,0},{32,56},{40,48},{48,40},{56,32},{64,88... | collective-permute-start | bytes 368648 | tf_op jit(solution)/shard_map/ppermute | solution.py:472
  15.5 5.5 %collective-permute-start.2 = (f32[3,5,16,128]{3,2,1,0:T(8,128)S(1)}, f32[3,5,16,128]{3,2,1,0:T(8,128)S(1)}, u32[]{:S(2)}, u32[]{:S(2)}) collective-permute-start(f32[3,5,16,128]{3,2,1,0:T(8,128)S(1)} %get-tuple-element.43.sent_ref), channel_id=1, source_target_pairs={{0,32},{8,40},{16,48},{24,56},{32,0},{40,8},{48,16},{56,24},{64,96... | collective-permute-start | bytes 368648 | tf_op jit(solution)/shard_map/ppermute | solution.py:497
  19.5 5.0 %collective-permute-start.4 = (f32[3,7680]{1,0:T(4,128)S(1)}, f32[3,7680]{1,0:T(4,128)S(1)}, u32[]{:S(2)}, u32[]{:S(2)}) collective-permute-start(f32[3,7680]{1,0:T(4,128)S(1)} %get-tuple-element.49.sent_ref), channel_id=1, source_target_pairs={{0,2},{2,0},{4,6},{6,4},{1,3},{3,1},{5,7},{7,5},{8,10},{10,8},{12,... | collective-permute-start | bytes 276488 | tf_op jit(solution)/shard_map/ppermute | solution.py:467
  21.1 11.9 %collective-permute-start.3 = (f32[2,5,16,128]{3,2,1,0:T(8,128)S(1)}, f32[2,5,16,128]{3,2,1,0:T(8,128)S(1)}, u32[]{:S(2)}, u32[]{:S(2)}) collective-permute-start(f32[2,5,16,128]{3,2,1,0:T(8,128)S(1)} %get-tuple-element.46), channel_id=1, source_target_pairs={{0,96},{8,104},{16,112},{24,120},{32,64},{40,72},{48,80},{56,88},{... | collective-permute-start | bytes 245768 | tf_op jit(solution)/shard_map/ppermute | solution.py:503
  24.5 5.8 %collective-permute-start.5 = (f32[2,7680]{1,0:T(2,128)S(1)}, f32[2,7680]{1,0:T(2,128)S(1)}, u32[]{:S(2)}, u32[]{:S(2)}) collective-permute-start(f32[2,7680]{1,0:T(2,128)S(1)} %get-tuple-element.53), channel_id=1, source_target_pairs={{0,6},{2,4},{4,2},{6,0},{1,7},{3,5},{5,3},{7,1},{8,14},{10,12},{12... | collective-permute-start | bytes 184328 | tf_op jit(solution)/shard_map/ppermute | solution.py:492

commit v4 on v3

--- a/solution.py
+++ b/solution.py
@@ -156,7 +156,8 @@
     return lax.dot_general(a, b, (dims, ((), ())), preferred_element_type=F32)
 
 
-READY = ((0,), (1,))
+READY = ((0, 1),)
+SPAN_ROWS = 1536
 STEP = 8
 
 
@@ -238,7 +239,8 @@
 
     for f in range(fields):
         high, mid, low = (
-            jnp.concatenate([ref[f, q] for q in range(planes)], axis=1) for ref in (high_ref, mid_ref, low_ref)
+            jnp.concatenate([ref[f, q * block : (q + 1) * block] for q in range(planes)], axis=1)
+            for ref in (high_ref, mid_ref, low_ref)
         )
         main = dot(lhs, jnp.concatenate([high, mid], axis=0), ((1,), (0,)))
         rest = dot(lhs2, jnp.concatenate([low, high], axis=0), ((1,), (0,)))
@@ -252,12 +254,12 @@
 def wall_final_kernel(
     local_ref, metric_ref, old_ref, got_ref, coef_ref, table_ref, tail_ref, span_in, out_hbm, span_hbm, buffer, sems
 ):
-    fields, planes, block, _ = local_ref.shape
+    fields, planes, block, lanes = local_ref.shape
     coef = coef_ref[...]
     table = table_ref[...].T[:block]
-    enter, leave = table[:, 2:3], table[:, 3:4]
-    top = lax.broadcasted_iota(jnp.int32, (1, 8, 1), 1) == 0
-    bottom = lax.broadcasted_iota(jnp.int32, (1, 8, 1), 1) == 7
+    enter, leave = (jnp.broadcast_to(table[:, j : j + 1], (block, lanes)) for j in (2, 3))
+    top = lax.broadcasted_iota(jnp.int32, (8, lanes), 0) == 0
+    bottom = lax.broadcasted_iota(jnp.int32, (8, lanes), 0) == 7
 
     def c(j):
         return coef[:, j : j + 1]
@@ -265,18 +267,20 @@
     copies = [pltpu.make_async_copy(tail_ref, span_hbm.at[fields - 1], sems.at[0])]
     copies[0].start()
     for f in range(fields):
-        for q in range(0, planes, STEP):
-            at = slice(q, q + STEP)
+        for start in range(0, planes, STEP):
+            at = slice(start, start + STEP)
             got, halo = got_ref[0, f, at], got_ref[1, f, at]
             m, n = old_ref[0, f, at] + c(24) * got, old_ref[1, f, at] + c(25) * got
             first, last = old_ref[2, f, at] + c(30) * halo, old_ref[3, f, at] + c(31) * halo
-            for lo, hi in ((0, 8), (8, block - 8), (block - 8, block)):
-                total = local_ref[f, at, lo:hi] + enter[None, lo:hi] * m[:, None, :] + leave[None, lo:hi] * n[:, None, :]
-                if lo == 0:
-                    total = total + jnp.where(top, first[:, None, :], 0.0)
-                if hi == block:
-                    total = total + jnp.where(bottom, last[:, None, :], 0.0)
-                buffer[f, at, lo:hi] = metric_ref[at, lo:hi] * total
+            for j in range(STEP):
+                q, row = start + j, slice(j, j + 1)
+                for lo, hi in ((0, 8), (8, block - 8), (block - 8, block)):
+                    total = local_ref[f, q, lo:hi] + (enter[lo:hi] * m[row] + leave[lo:hi] * n[row])
+                    if lo == 0:
+                        total = total + jnp.where(top, first[row], 0.0)
+                    if hi == block:
+                        total = total + jnp.where(bottom, last[row], 0.0)
+                    buffer[f, q, lo:hi] = metric_ref[q, lo:hi] * total
             copies.append(pltpu.make_async_copy(buffer.at[f, at], out_hbm.at[f, at], sems.at[len(copies)]))
             copies[-1].start()
     for copy in copies:
@@ -289,17 +293,19 @@
     table = table_ref[...]
     lines = planes * rows
     for f in range(fields):
-        at = slice(f * lines, (f + 1) * lines)
-        high, mid, low = split_parts(x_ref[f].reshape(lines, columns))
-        for ref, part in ((high_ref, high), (mid_ref, mid), (low_ref, low)):
-            ref[f] = part.reshape(planes, rows, columns)
-        main = dot(table[:16], jnp.concatenate([high, mid], axis=1), ((1,), (1,)))
-        rest = dot(table[16:], jnp.concatenate([low, high], axis=1), ((1,), (1,)))
-        total = main[:8] + (main[8:] + rest[:8])
-        first, last = total[2:3], total[3:4]
-        pay_ref[0:2, at] = total[0:2]
-        pay_ref[2:3, at] = jnp.where(even, last, first)
-        other_ref[:, at] = jnp.where(even, first, last)
+        flat = x_ref[f].reshape(lines, columns)
+        for start in range(0, lines, SPAN_ROWS):
+            inside = slice(start, start + SPAN_ROWS)
+            high, mid, low = split_parts(flat[inside])
+            high_ref[f, inside], mid_ref[f, inside], low_ref[f, inside] = high, mid, low
+            main = dot(table, jnp.concatenate([high, mid], axis=1), ((1,), (1,)))
+            rest = dot(table[:16, :columns], low, ((1,), (1,)))
+            total = main[:8] + (main[8:16] + (main[16:24] + rest[:8]))
+            first, last = total[2:3], total[3:4]
+            at = slice(f * lines + start, f * lines + start + SPAN_ROWS)
+            pay_ref[0:2, at] = total[0:2]
+            pay_ref[2:3, at] = jnp.where(even, last, first)
+            other_ref[:, at] = jnp.where(even, first, last)
 
 
 def span_matrices(table):
@@ -321,8 +327,7 @@
     count, planes, rows, n = out_ref.shape
     weights = span_matrices(table_ref[...])
     for j in range(count):
-        parts = (ref[start + j].reshape(planes * rows, n) for ref in (high_ref, mid_ref, low_ref))
-        a, b = span_product(weights, *parts)
+        a, b = span_product(weights, *(ref[start + j] for ref in (high_ref, mid_ref, low_ref)))
         out_ref[j] = (a + b).reshape(planes, rows, n)
 
 
@@ -344,7 +349,8 @@
 def span_final_kernel(ready, high_ref, mid_ref, low_ref, metric_ref, old_ref, got_ref, coef_ref, table_ref, edge_ref, *refs):
     locals_ref = refs[: len(ready)]
     out_hbm, tail_ref, buffer, sems = refs[len(ready) :]
-    fields, planes, rows, n = high_ref.shape
+    planes, rows, n = metric_ref.shape
+    fields = high_ref.shape[0]
     coef = coef_ref[...]
     weights = span_matrices(table_ref[...])
 
@@ -371,7 +377,7 @@
             ref, j = own[f]
             total = ref[j].reshape(lines, n) + edge
         else:
-            a, b = span_product(weights, *(ref[f].reshape(lines, n) for ref in (high_ref, mid_ref, low_ref)))
+            a, b = span_product(weights, *(ref[f] for ref in (high_ref, mid_ref, low_ref)))
             total = a + (b + edge)
         total = metric_ref[...] * total.reshape(planes, rows, n)
         if f == fields - 1:
@@ -423,7 +429,7 @@
     span_pick = np.zeros((span_pieces, 32, 2 * columns), BF16)
     span_pick[:, 0:4] = np.concatenate([p_high, p_high], axis=2)
     span_pick[:, 8:12] = np.concatenate([p_mid, p_mid], axis=2)
-    span_pick[:, 16:20] = np.concatenate([p_high, p_low], axis=2)
+    span_pick[:, 16:20, :columns] = p_low
     spread = np.zeros((span_pieces, 8, columns))
     spread[:, 0], spread[:, 1] = st["enter"], st["leave"]
     spread[:, 2, 0] = 1.0
@@ -437,9 +443,14 @@
         out[:, 0, : c.shape[1]] = c
         return out
 
+    def at_hbm(values):
+        return [pltpu.with_memory_space_constraint(jnp.asarray(t), pltpu.HBM) for t in values]
+
+    def one(values):
+        return [shape(*t.shape[1:], dtype=t.dtype) for t in values]
+
     tables = [wall_rows, wall_diag, spread_coefficients(wt, wall_pieces)]
-    tables += [span_diag, span_pick, span_edge, spread_coefficients(st, span_pieces)]
-    tables = [pltpu.with_memory_space_constraint(jnp.asarray(t), pltpu.HBM) for t in tables]
+    tables = at_hbm(tables + [span_diag, span_pick, span_edge, spread_coefficients(st, span_pieces)])
     grid_values = pltpu.with_memory_space_constraint(conserved, pltpu.HBM)
 
     state = shape(4, fields, planes, columns)
@@ -448,8 +459,7 @@
         wall_moment_kernel,
         [hbm] * 8,
         [vmem] * 10,
-        [shape(*t.shape[1:], dtype=t.dtype) for t in tables]
-        + [shape(*conserved.shape), moment, shape(fields, planes, columns)],
+        one(tables) + [shape(*conserved.shape), moment, shape(fields, planes, columns)],
         2.5,
         [pltpu.SemaphoreType.DMA((chunks,)), pltpu.SemaphoreType.DMA((len(tables),))],
     )(grid_values, *tables)
@@ -460,9 +470,9 @@
 
     got_w = lax.ppermute(pay_w, "wall", swap(1, wall_pieces))
 
-    part = shape(*conserved.shape, dtype=BF16)
+    part = shape(fields, planes * rows, columns, dtype=BF16)
     pay_s, other_s, *parts = call(
-        span_moment_kernel, [vmem] * 2, [vmem] * 5, [shape(3, lines), shape(1, lines)] + [part] * 3, 2.1
+        span_moment_kernel, [vmem] * 2, [vmem] * 5, [shape(3, lines), shape(1, lines)] + [part] * 3, 2.0
     )(x, s_pick)
     got_s = lax.ppermute(pay_s, "span", swap(1, span_pieces))
 

time: 35.6 us -> 34.9 us (0.980)
  Pallas kernels: 13.1 us -> 12.4 us
    pallas_call x2 -> x1, Pallas kernels: 1.14 us -> 0.99 us  [span_local(): call(functools.partial(span_local_kernel, group[0]), [vmem] * 4, vmem, sh...]
  transfers between devices with their start and end apart: 6 -> 6, of which waited for: 3 -> 3; matrix products, arithmetic and copies ran while one was open for 0% -> 0% of each run, Pallas kernels for 23% -> 22%
where the time goes in v4:
time: 34.9 us; the launch traced here: 34.8 us
  starting transfers between devices  15 us (43%)
  Pallas kernels  12.4 us (36%)
  waiting for transfers between devices  6.63 us (19%)
  between operations  0.71 us (2%)
    ppermute x1, starting transfers between devices, slopes(): got_w = lax.ppermute(pay_w, 'wall', swap(3, wall_pieces))  3.96 us
    ppermute x1, waiting for transfers between devices, slopes(): got_w = lax.ppermute(pay_w, 'wall', swap(1, wall_pieces))  3.32 us
    ppermute x1, waiting for transfers between devices, slopes(): got_w = lax.ppermute(pay_w, 'wall', swap(3, wall_pieces))  2.86 us
    ppermute x1, starting transfers between devices, slopes(): got_w = lax.ppermute(pay_w, 'wall', swap(12, wall_pieces))  2.84 us
    ppermute x1, starting transfers between devices, slopes(): got_s = lax.ppermute(pay_s, 'span', swap(3, span_pieces))  2.84 us
    pallas_call x1, Pallas kernels, slopes(): call(functools.partial(span_final_kernel, READY), [vmem] * (9 + len(READY...  2.7 us
    pallas_call x1, Pallas kernels, slopes(): call(wall_moment_kernel, [hbm] * 8, [vmem] * 10, one(tables) + [shape(*co...  2.48 us
    pallas_call x1, Pallas kernels, slopes(): call(wall_final_kernel, [vmem] * 7 + [hbm], [hbm] * 2, [shape(*conserved....  2.27 us
  transfers between devices with their start and end apart: 6, of which 3 were waited for; matrix products, arithmetic and copies ran while one was open for 0% of the time, Pallas kernels for 22%

profile of v4, /device:TPU:0, one launch (start us, length us, event | category | flops | bytes accessed | tf_op | source)
XLA Modules:
  0.0 34.8 jit_solution(2632047039405388656)
XLA Ops:
  0.6 2.5 %shard_map.113 = (f32[8,128]{1,0:T(8,128)S(1)}, bf16[288,128]{1,0:T(8,128)(2,1)S(1)}, f32[1,128]{1,0:T(1,128)S(1)}, bf16[128,384]{1,0:T(8,128)(2,1)S(1)}, bf16[3...) custom-call(f32[5,16,96,128]{3,2,1,0:T(8,128)} %x_hbm.1, ...), custom_call_target="tpu_custom_call" | custom-call | bytes 7500000 | tf_op jit(solution)/shard_map/pallas_call | solution.py:458
  3.1 2.1 %collective-permute-start = (f32[3,5,16,128]{3,2,1,0:T(8,128)S(1)}, f32[3,5,16,128]{3,2,1,0:T(8,128)S(1)}, u32[]{:S(2)}, u32[]{:S(2)}) collective-permute-start(f32[3,5,16,128]{3,2,1,0:T(8,128)S(1)} %get-tuple-element.38.sent_ref), channel_id=1, source_target_pairs={{0,8},{8,0},{16,24},{24,16},{32,40},{40,32},{48,56},{56,48},{64,72... | collective-permute-start | bytes 368648 | tf_op jit(solution)/shard_map/ppermute | solution.py:471
  5.2 3.3 %collective-permute-done.got_ref = f32[3,5,16,128]{3,2,1,0:T(8,128)S(1)} collective-permute-done((f32[3,5,16,128]{3,2,1,0:T(8,128)S(1)}, f32[3,5,16,128]{3,2,1,0:T(8,128)S(1)}, u32[]{:S(2)}, u32[]{:S(2)}) %collective-permute-start) | collective-permute-done | bytes 122912 | tf_op jit(solution)/shard_map/ppermute | solution.py:471
  8.5 0.1 shard_map.116
  8.6 4.0 %collective-permute-start.1 = (f32[3,5,16,128]{3,2,1,0:T(8,128)S(1)}, f32[3,5,16,128]{3,2,1,0:T(8,128)S(1)}, u32[]{:S(2)}, u32[]{:S(2)}) collective-permute-start(f32[3,5,16,128]{3,2,1,0:T(8,128)S(1)} %get-tuple-element.41.sent_ref), channel_id=1, source_target_pairs={{0,24},{8,16},{16,8},{24,0},{32,56},{40,48},{48,40},{56,32},{64,88... | collective-permute-start | bytes 368648 | tf_op jit(solution)/shard_map/ppermute | solution.py:482
  12.6 2.9 %collective-permute-done.1.got_ref = f32[3,5,16,128]{3,2,1,0:T(8,128)S(1)} collective-permute-done((f32[3,5,16,128]{3,2,1,0:T(8,128)S(1)}, f32[3,5,16,128]{3,2,1,0:T(8,128)S(1)}, u32[]{:S(2)}, u32[]{:S(2)}) %collective-permute-start.1) | collective-permute-done | bytes 122912 | tf_op jit(solution)/shard_map/ppermute | solution.py:482
  15.4 0.1 shard_map.117
  15.5 1.7 %collective-permute-start.2 = (f32[3,5,16,128]{3,2,1,0:T(8,128)S(1)}, f32[3,5,16,128]{3,2,1,0:T(8,128)S(1)}, u32[]{:S(2)}, u32[]{:S(2)}) collective-permute-start(f32[3,5,16,128]{3,2,1,0:T(8,128)S(1)} %get-tuple-element.43.sent_ref), channel_id=1, source_target_pairs={{0,32},{8,40},{16,48},{24,56},{32,0},{40,8},{48,16},{56,24},{64,96... | collective-permute-start | bytes 368648 | tf_op jit(solution)/shard_map/ppermute | solution.py:507
  17.2 1.9 %shard_map.114 = (f32[3,7680]{1,0:T(4,128)S(1)}, f32[1,7680]{1,0:T(1,128)S(1)}, bf16[5,1536,128]{2,1,0:T(8,128)(2,1)S(1)}, bf16[5,1536,128]{2,1,0:T(8,128)(2,1)S(1)}, bf16[5,1536,128]{2,1,0:T(8,128)(2,1)S(1)}) custom-call(f32[5,16,96,128]{3,2,1,0:T(8,128)S(1)} %get-tuple-element.30.x_ref, bf16[32,256]{1,0:T(8,128)(2,1)S(1)} %get-tuple-element.31.table_ref), custom_call_target="tpu_custom_call" | custom-call | bytes 6000000 | tf_op jit(solution)/shard_map/pallas_call | solution.py:474
  19.1 1.6 %collective-permute-start.4 = (f32[3,7680]{1,0:T(4,128)S(1)}, f32[3,7680]{1,0:T(4,128)S(1)}, u32[]{:S(2)}, u32[]{:S(2)}) collective-permute-start(f32[3,7680]{1,0:T(4,128)S(1)} %get-tuple-element.49.sent_ref), channel_id=1, source_target_pairs={{0,2},{2,0},{4,6},{6,4},{1,3},{3,1},{5,7},{7,5},{8,10},{10,8},{12,... | collective-permute-start | bytes 276488 | tf_op jit(solution)/shard_map/ppermute | solution.py:477
  20.7 0.0 collective-permute-done.2.got_ref
  20.7 0.1 shard_map.118
  20.8 2.8 %collective-permute-start.3 = (f32[2,5,16,128]{3,2,1,0:T(8,128)S(1)}, f32[2,5,16,128]{3,2,1,0:T(8,128)S(1)}, u32[]{:S(2)}, u32[]{:S(2)}) collective-permute-start(f32[2,5,16,128]{3,2,1,0:T(8,128)S(1)} %get-tuple-element.46), channel_id=1, source_target_pairs={{0,96},{8,104},{16,112},{24,120},{32,64},{40,72},{48,80},{56,88},{... | collective-permute-start | bytes 245768 | tf_op jit(solution)/shard_map/ppermute | solution.py:513
  23.6 0.4 %collective-permute-done.4.got_ref = f32[3,7680]{1,0:T(4,128)S(1)} collective-permute-done((f32[3,7680]{1,0:T(4,128)S(1)}, f32[3,7680]{1,0:T(4,128)S(1)}, u32[]{:S(2)}, u32[]{:S(2)}) %collective-permute-start.4) | collective-permute-done | bytes 92192 | tf_op jit(solution)/shard_map/ppermute | solution.py:477
  24.1 0.1 shard_map.119
  24.2 2.8 %collective-permute-start.5 = (f32[2,7680]{1,0:T(2,128)S(1)}, f32[2,7680]{1,0:T(2,128)S(1)}, u32[]{:S(2)}, u32[]{:S(2)}) collective-permute-start(f32[2,7680]{1,0:T(2,128)S(1)} %get-tuple-element.53), channel_id=1, source_target_pairs={{0,6},{2,4},{4,2},{6,0},{1,7},{3,5},{5,3},{7,1},{8,14},{10,12},{12... | collective-permute-start | bytes 184328 | tf_op jit(solution)/shard_map/ppermute | solution.py:502
  27.0 1.0 %shard_map.120.refs_0_ = f32[2,16,96,128]{3,2,1,0:T(8,128)S(1)} custom-call(bf16[5,1536,128]{2,1,0:T(8,128)(2,1)S(1)} %get-tuple-element.32.high_ref, bf16[5,1536,128]{2,1,0:T(8,128)(2,1)S(1)} %get-tuple-element.33.mid_ref, bf16[5,1536,128]{2,1,0:T(8,128)(2,1)S(1)} %get-tuple-element.34.low_ref, bf16[128,384]{1,0:T(8,128)(2,1)S(1)} %get-tuple-element.54.table_ref), custom_call_target="tpu_custom_call" | custom-call | bytes 3600000 | tf_op jit(solution)/shard_map/pallas_call | solution.py:492
  28.0 1.8 %shard_map.115 = (f32[5,16,96,128]{3,2,1,0:T(8,128)S(1)}, f32[16,96,128]{2,1,0:T(8,128)S(1)}, f32[16,96,128]{2,1,0:T(8,128)S(1)}) custom-call(bf16[5,1536,128]{2,1,0:T(8,128)(2,1)S(1)} %get-tuple-element.32.high_ref, bf16[5,1536,128]{2,1,0:T(8,128)(2,1)S(1)} %get-tuple-element.33.mid_ref, bf16[5,1536,128]{2,1,0:T(8,128)(2,1)S(1)} %get-tuple-element.34.low_ref, ...), custom_call_target="tpu_custom_call" | custom-call | bytes 5100000 | tf_op jit(solution)/shard_map/pallas_call | solution.py:485
  29.8 0.0 collective-permute-done.5.got_ref
  29.8 2.7 %shard_map.121 = (f32[5,16,96,128]{3,2,1,0:T(8,128)}, f32[16,96,128]{2,1,0:T(8,128)S(1)}) custom-call(bf16[5,1536,128]{2,1,0:T(8,128)(2,1)S(1)} %get-tuple-element.32.high_ref, bf16[5,1536,128]{2,1,0:T(8,128)(2,1)S(1)} %get-tuple-element.33.mid_ref, bf16[5,1536,128]{2,1,0:T(8,128)(2,1)S(1)} %get-tuple-element.34.low_ref, ...), custom_call_target="tpu_custom_call" | custom-call | bytes 9000000 | tf_op jit(solution)/shard_map/pallas_call | solution.py:515
  32.5 0.0 collective-permute-done.3.got_ref
  32.5 2.3 %shard_map.122 = (f32[5,16,96,128]{3,2,1,0:T(8,128)}, f32[5,16,96,128]{3,2,1,0:T(8,128)}) custom-call(f32[5,16,96,128]{3,2,1,0:T(8,128)S(1)} %get-tuple-element.36.local_ref, f32[16,96,128]{2,1,0:T(8,128)S(1)} %get-tuple-element.37.metric_ref, f32[4,5,16,128]{3,2,1,0:T(8,128)S(1)} %get-tuple-element.45.old_ref, ...), custom_call_target="tpu_custom_call", output_to_operand_aliasing={{1}: (7, {})} | custom-call | bytes 7200000 | tf_op jit(solution)/shard_map/pallas_call | solution.py:520
  (1 shorter events, 0.0 us)
Async XLA Ops:
  3.1 5.4 %collective-permute-start = (f32[3,5,16,128]{3,2,1,0:T(8,128)S(1)}, f32[3,5,16,128]{3,2,1,0:T(8,128)S(1)}, u32[]{:S(2)}, u32[]{:S(2)}) collective-permute-start(f32[3,5,16,128]{3,2,1,0:T(8,128)S(1)} %get-tuple-element.38.sent_ref), channel_id=1, source_target_pairs={{0,8},{8,0},{16,24},{24,16},{32,40},{40,32},{48,56},{56,48},{64,72... | collective-permute-start | bytes 368648 | tf_op jit(solution)/shard_map/ppermute | solution.py:471
  8.6 6.8 %collective-permute-start.1 = (f32[3,5,16,128]{3,2,1,0:T(8,128)S(1)}, f32[3,5,16,128]{3,2,1,0:T(8,128)S(1)}, u32[]{:S(2)}, u32[]{:S(2)}) collective-permute-start(f32[3,5,16,128]{3,2,1,0:T(8,128)S(1)} %get-tuple-element.41.sent_ref), channel_id=1, source_target_pairs={{0,24},{8,16},{16,8},{24,0},{32,56},{40,48},{48,40},{56,32},{64,88... | collective-permute-start | bytes 368648 | tf_op jit(solution)/shard_map/ppermute | solution.py:482
  15.5 5.2 %collective-permute-start.2 = (f32[3,5,16,128]{3,2,1,0:T(8,128)S(1)}, f32[3,5,16,128]{3,2,1,0:T(8,128)S(1)}, u32[]{:S(2)}, u32[]{:S(2)}) collective-permute-start(f32[3,5,16,128]{3,2,1,0:T(8,128)S(1)} %get-tuple-element.43.sent_ref), channel_id=1, source_target_pairs={{0,32},{8,40},{16,48},{24,56},{32,0},{40,8},{48,16},{56,24},{64,96... | collective-permute-start | bytes 368648 | tf_op jit(solution)/shard_map/ppermute | solution.py:507
  19.1 5.0 %collective-permute-start.4 = (f32[3,7680]{1,0:T(4,128)S(1)}, f32[3,7680]{1,0:T(4,128)S(1)}, u32[]{:S(2)}, u32[]{:S(2)}) collective-permute-start(f32[3,7680]{1,0:T(4,128)S(1)} %get-tuple-element.49.sent_ref), channel_id=1, source_target_pairs={{0,2},{2,0},{4,6},{6,4},{1,3},{3,1},{5,7},{7,5},{8,10},{10,8},{12,... | collective-permute-start | bytes 276488 | tf_op jit(solution)/shard_map/ppermute | solution.py:477
  20.8 11.7 %collective-permute-start.3 = (f32[2,5,16,128]{3,2,1,0:T(8,128)S(1)}, f32[2,5,16,128]{3,2,1,0:T(8,128)S(1)}, u32[]{:S(2)}, u32[]{:S(2)}) collective-permute-start(f32[2,5,16,128]{3,2,1,0:T(8,128)S(1)} %get-tuple-element.46), channel_id=1, source_target_pairs={{0,96},{8,104},{16,112},{24,120},{32,64},{40,72},{48,80},{56,88},{... | collective-permute-start | bytes 245768 | tf_op jit(solution)/shard_map/ppermute | solution.py:513
  24.2 5.6 %collective-permute-start.5 = (f32[2,7680]{1,0:T(2,128)S(1)}, f32[2,7680]{1,0:T(2,128)S(1)}, u32[]{:S(2)}, u32[]{:S(2)}) collective-permute-start(f32[2,7680]{1,0:T(2,128)S(1)} %get-tuple-element.53), channel_id=1, source_target_pairs={{0,6},{2,4},{4,2},{6,0},{1,7},{3,5},{5,3},{7,1},{8,14},{10,12},{12... | collective-permute-start | bytes 184328 | tf_op jit(solution)/shard_map/ppermute | solution.py:502
